TPU v7x, 512 devices: a whole 4x4x16 slice. The times are simulated.
512 devices in a mesh: segment: 4 (over x), rep: 8 (over y, core), box: 16 (over z).
Axes of the slice: x: 4, y: 4, z: 16, core: 2. Of those that a mesh axis runs over, the one named last changes fastest.
Arguments:
- centers: float32 [512, 4, 4, 512], P(('rep', 'box')), may hold values from -6 to 6
- box_radii: float32 [512, 4, 4, 512], P(('rep', 'box')), may hold values from 0.001 to 0.01
- labels: int32 [512], P(('rep', 'box')), may hold values from 0 to 9
- certified: int32 [512], P(('rep', 'box')), may hold values from 0 to 1, as said below
- conv_weights: bfloat16 [4, 9, 512, 512], P('segment', None, 'box'), may hold values from -0.01171875 to 0.01171875
- conv_bias: float32 [4, 512], P('segment'), may hold values from -1.2 to 1.2
- head_weight: bfloat16 [512, 10], replicated, may hold values from -0.25 to 0.25
- head_bias: float32 [10], replicated, may hold values from -4 to 4
Outputs:
- lower_bounds: float32 [128, 4, 5], P(('rep', 'box'), 'segment')
Inputs may be any that keep to these rules, and one draw needn't show every extreme that they name: `certified`: for each box index and each i, the devices 2i and 2i + 1 along rep hold 4 boxes with value 0 together; in each box index some such pair has all 4 of them on one device.
All inputs are finite; a program needn't handle non-finite values.
Results may differ from a plain program's by a relative error of at most 0.00055.
Values may be sent and summed in bfloat16 or wider, within the bound.
A program may use at most 64 MiB of HBM per device.

v0:
```python
import jax
import jax.numpy as jnp
from jax import lax
from jax.sharding import PartitionSpec as P

K = 5
MICRO = 2


highest = lax.Precision.HIGHEST


def shifted(x, axis, by):
    count = lax.axis_size(axis)
    pairs = [(i, i + by) for i in range(count) if 0 <= i + by < count]
    return lax.ppermute(x, axis, pairs)


def partner(value, axis, apart):
    mask = 2**apart
    pairs = [(source, source ^ mask) for source in range(lax.axis_size(axis))]
    return lax.ppermute(value, axis, pairs)


def in_blocks(x, dim, count):
    lengths = x.shape
    parts = x.reshape(*lengths[:dim], count, lengths[dim] // count, *lengths[dim + 1 :])
    return jnp.moveaxis(parts, dim, 0)


def summed_on_arrival(x, axis, dim):
    count = lax.axis_size(axis)
    parts = lax.all_to_all(in_blocks(x, dim, count), axis, 0, 0, tiled=True)
    return jnp.sum(parts, axis=0)


def convolve(values, kernel_cols):
    extent = values.shape[1]
    padded = jnp.pad(values, ((0, 0), (1, 1), (1, 1), (0, 0)))
    windows = []
    for tap_index in range(9):
        row_shift, col_shift = divmod(tap_index, 3)
        windows.append(padded[:, row_shift : row_shift + extent, col_shift : col_shift + extent, :])
    stacked = jnp.concatenate(windows, axis=3)
    return lax.dot_general(
        stacked, kernel_cols, (((3,), (0,)), ((), ())), preferred_element_type=jnp.float32
    )


def convolve_back(gradient, kernel_rows):
    extent = gradient.shape[1]
    padded = jnp.pad(gradient, ((0, 0), (1, 1), (1, 1), (0, 0)))
    windows = []
    for tap_index in range(9):
        row_shift, col_shift = divmod(tap_index, 3)
        windows.append(
            padded[
                :, 2 - row_shift : 2 - row_shift + extent, 2 - col_shift : 2 - col_shift + extent, :
            ]
        )
    stacked = jnp.concatenate(windows, axis=3)
    return lax.dot_general(
        stacked, kernel_rows, (((3,), (0,)), ((), ())), preferred_element_type=jnp.float32
    )


def forward_layer(middle, radius, kernel_cols, magnitude_cols, shift_bias):
    centre = convolve(middle.astype(jnp.bfloat16), kernel_cols) + shift_bias
    spread = convolve(radius.astype(jnp.bfloat16), magnitude_cols)
    lower_edge = centre - spread
    upper_edge = centre + spread
    upper_pos = jax.nn.relu(upper_edge)
    lower_neg = jax.nn.relu(-lower_edge)
    lower_pos = jax.nn.relu(lower_edge)
    slope_now = upper_pos / (upper_pos + lower_neg)
    intercept = slope_now * lower_neg
    middle = middle + 0.5 * (upper_pos + lower_pos)
    radius = radius + 0.5 * (upper_pos - lower_pos)
    return (middle, radius, slope_now, intercept)


def backward_layer(coeffs, slope_now, intercept, kernel_rows, shift_bias):
    scaled = coeffs * slope_now[:, None]
    layer_term = jnp.sum(
        scaled * shift_bias + jnp.minimum(coeffs, 0.0) * intercept[:, None], axis=(2, 3, 4)
    )
    gradient = scaled.astype(jnp.bfloat16).reshape((-1,) + scaled.shape[2:])
    coeffs = coeffs + convolve_back(gradient, kernel_rows).reshape(coeffs.shape)
    return (coeffs, layer_term)


def head_coeffs(label_box, head_weight, head_bias, extent, channels):
    classes = head_bias.shape[0]
    spec_rows = jnp.arange(K, dtype=jnp.int32)[None, :]
    others = (label_box[:, None] + 1 + spec_rows) % classes
    class_ids = jnp.arange(classes, dtype=jnp.int32)
    selector = (class_ids[None, None, :] == label_box[:, None, None]).astype(jnp.float32) - (
        class_ids[None, None, :] == others[:, :, None]
    ).astype(jnp.float32)
    pooled = jnp.einsum(
        "bkc,fc->bkf", selector, head_weight.astype(jnp.float32), precision=highest
    ) / float(extent * extent)
    offset = jnp.einsum("bkc,c->bk", selector, head_bias, precision=highest)
    coeffs = jnp.broadcast_to(
        pooled[:, :, None, None, :], (label_box.shape[0], K, extent, extent, channels)
    )
    return (coeffs, offset)


def concretize(coeffs, centre_box, radius_box):
    return jnp.sum(
        coeffs * centre_box[:, None] - jnp.abs(coeffs) * radius_box[:, None], axis=(2, 3, 4)
    )


def run_sections(
    centres,
    radii_in,
    labels_in,
    conv_weights,
    conv_bias,
    head_weight,
    head_bias,
    segment_index,
    segment_count,
):
    rows_total = centres.shape[0]
    micro_rows = rows_total // MICRO
    extent = centres.shape[1]
    channels = centres.shape[3]
    kernel = lax.all_gather(conv_weights, "box", axis=2, tiled=True)[0]
    kernel_cols = jnp.transpose(kernel, (0, 2, 1)).reshape(9 * channels, channels)
    magnitude_cols = jnp.abs(kernel_cols)
    shift_bias = conv_bias[0]
    steps_total = MICRO + segment_count - 1
    at_first = segment_index == 0
    at_last = segment_index == segment_count - 1
    block_shape = (micro_rows, extent, extent, channels)
    slopes = jnp.zeros(centres.shape, jnp.float32)
    intercepts = jnp.zeros(centres.shape, jnp.float32)
    incoming = (jnp.zeros(block_shape, jnp.float32), jnp.zeros(block_shape, jnp.float32))

    def section_forward(operands):
        return forward_layer(operands[0], operands[1], kernel_cols, magnitude_cols, shift_bias)

    def spare_forward(operands):
        return (operands[0], operands[1], jnp.zeros_like(operands[0]), jnp.zeros_like(operands[0]))

    for step_index in range(steps_total):
        micro_index = step_index - segment_index
        active = (micro_index >= 0) & (micro_index < MICRO)
        row_start = jnp.clip(micro_index, 0, MICRO - 1) * micro_rows
        own_middle = lax.dynamic_slice_in_dim(centres, row_start, micro_rows, 0)
        own_radius = lax.dynamic_slice_in_dim(radii_in, row_start, micro_rows, 0)
        middle = jnp.where(at_first, own_middle, incoming[0])
        radius = jnp.where(at_first, own_radius, incoming[1])
        new_middle, new_radius, slope_now, intercept = lax.cond(
            active, section_forward, spare_forward, (middle, radius)
        )
        old_slope = lax.dynamic_slice_in_dim(slopes, row_start, micro_rows, 0)
        old_intercept = lax.dynamic_slice_in_dim(intercepts, row_start, micro_rows, 0)
        slopes = lax.dynamic_update_slice_in_dim(
            slopes, jnp.where(active, slope_now, old_slope), row_start, 0
        )
        intercepts = lax.dynamic_update_slice_in_dim(
            intercepts, jnp.where(active, intercept, old_intercept), row_start, 0
        )
        if step_index < steps_total - 1:
            incoming = (
                shifted(new_middle.astype(jnp.bfloat16), "segment", 1).astype(new_middle.dtype),
                shifted(new_radius.astype(jnp.bfloat16), "segment", 1).astype(new_radius.dtype),
            )
    kernel = lax.all_gather(conv_weights, "box", axis=2, tiled=True)[0]
    kernel_rows = kernel.reshape(9 * channels, channels)

    def section_back(operands):
        coeffs, slope_block, intercept_block, centre_block, radius_block, offset = operands
        new_coeffs, layer_term = backward_layer(
            coeffs, slope_block, intercept_block, kernel_rows, shift_bias
        )
        layer_term = layer_term + jnp.where(at_last, offset, 0.0)
        layer_term = layer_term + jnp.where(
            at_first, concretize(new_coeffs, centre_block, radius_block), 0.0
        )
        return (new_coeffs, layer_term)

    def spare_back(operands):
        return (operands[0], jnp.zeros_like(operands[5]))

    contrib = jnp.zeros((rows_total, K), jnp.float32)
    arriving = jnp.zeros((micro_rows, K, extent, extent, channels), jnp.bfloat16)
    for step_index in range(steps_total):
        micro_index = step_index - (segment_count - 1 - segment_index)
        active = (micro_index >= 0) & (micro_index < MICRO)
        row_start = jnp.clip(micro_index, 0, MICRO - 1) * micro_rows
        label_block = lax.dynamic_slice_in_dim(labels_in, row_start, micro_rows, 0)
        head_part, offset = head_coeffs(label_block, head_weight, head_bias, extent, channels)
        coeffs = jnp.where(at_last, head_part, arriving.astype(jnp.float32))
        operands = (
            coeffs,
            lax.dynamic_slice_in_dim(slopes, row_start, micro_rows, 0),
            lax.dynamic_slice_in_dim(intercepts, row_start, micro_rows, 0),
            lax.dynamic_slice_in_dim(centres, row_start, micro_rows, 0),
            lax.dynamic_slice_in_dim(radii_in, row_start, micro_rows, 0),
            offset,
        )
        new_coeffs, layer_term = lax.cond(active, section_back, spare_back, operands)
        old_term = lax.dynamic_slice_in_dim(contrib, row_start, micro_rows, 0)
        contrib = lax.dynamic_update_slice_in_dim(
            contrib, jnp.where(active, layer_term, old_term), row_start, 0
        )
        if step_index < steps_total - 1:
            arriving = shifted(new_coeffs.astype(jnp.bfloat16), "segment", -1)
    return contrib


def per_device(
    centers, box_radii, labels, certified, conv_weights, conv_bias, head_weight, head_bias
):
    segment_count = lax.axis_size("segment")
    segment_index = lax.axis_index("segment")
    box_count = centers.shape[0]
    alive_rows = 1 - certified
    half_rows = box_count // 2
    tail_shape = centers.shape[1:]
    live_rank = jnp.cumsum(alive_rows) - alive_rows
    own_total = jnp.sum(alive_rows)
    slots = jnp.arange(half_rows, dtype=jnp.int32)
    is_live = alive_rows[None, :] > 0
    keep_map = ((slots[:, None] == live_rank[None, :]) & is_live).astype(jnp.float32)
    send_map = ((slots[:, None] + half_rows == live_rank[None, :]) & is_live).astype(jnp.float32)
    fill_map = (slots[:, None] == own_total + slots[None, :]).astype(jnp.float32)
    flat_centres = centers.reshape(box_count, -1)
    flat_radii = box_radii.reshape(box_count, -1)
    label_tags = (labels + 1).astype(jnp.float32)[:, None]
    got_centres, got_radii, got_tags = partner(
        (
            jnp.dot(send_map, flat_centres, precision=highest),
            jnp.dot(send_map, flat_radii, precision=highest),
            jnp.dot(send_map, label_tags, precision=highest),
        ),
        "rep",
        0,
    )
    work_centres = (
        jnp.dot(keep_map, flat_centres, precision=highest)
        + jnp.dot(fill_map, got_centres, precision=highest)
    ).reshape((half_rows,) + tail_shape)
    work_radii = (
        jnp.dot(keep_map, flat_radii, precision=highest)
        + jnp.dot(fill_map, got_radii, precision=highest)
    ).reshape((half_rows,) + tail_shape)
    work_tags = jnp.dot(keep_map, label_tags, precision=highest) + jnp.dot(
        fill_map, got_tags, precision=highest
    )
    work_labels = jnp.maximum(work_tags[:, 0].astype(jnp.int32) - 1, 0)
    contrib = run_sections(
        work_centres,
        work_radii,
        work_labels,
        conv_weights,
        conv_bias,
        head_weight,
        head_bias,
        segment_index,
        segment_count,
    )
    outgoing = jnp.dot(fill_map.T, contrib, precision=highest)
    returned = partner(outgoing, "rep", 0)
    per_box = jnp.dot(keep_map.T, contrib, precision=highest) + jnp.dot(
        send_map.T, returned, precision=highest
    )
    summed = summed_on_arrival(per_box, "segment", 0)
    return summed[None]


def solution(mesh):
    placed = (
        P(("rep", "box"), None, None, None),
        P(("rep", "box"), None, None, None),
        P(("rep", "box")),
        P(("rep", "box")),
        P("segment", None, "box", None),
        P("segment", None),
        P(),
        P(),
    )
    return jax.shard_map(
        per_device,
        mesh=mesh,
        in_specs=placed,
        out_specs=P(("rep", "box"), "segment", None),
        check_vma=False,
    )
```

profile of v0, /device:TPU:1, one launch (start us, length us, event | category | flops | bytes accessed | tf_op | source)
XLA Modules:
  0.0 220.3 jit_solution(12544865204578964342)
XLA Ops:
  9.8 1.3 fusion.186
  11.4 8.7 %collective-permute-start.1 = (f32[2,8192]{1,0:T(2,128)S(1)}, f32[2,8192]{1,0:T(2,128)S(1)}, u32[]{:S(2)}, u32[]{:S(2)}) collective-permute-start(f32[2,8192]{1,0:T(2,128)S(1)} %fusion.194), channel_id=1, source_target_pairs={{0,16},{16,0},{32,48},{48,32},{64,80},{80,64},{96,112},{112,96},{1... | collective-permute-start | bytes 196616 | tf_op jit(solution)/shard_map/ppermute | solution.py:22
  21.4 1.9 collective-permute-start.2
  23.5 2.4 %collective-permute-start = (f32[2,1]{0,1:T(1,128)S(1)}, f32[2,1]{0,1:T(1,128)S(1)}, u32[]{:S(2)}, u32[]{:S(2)}) collective-permute-start(f32[2,1]{0,1:T(1,128)S(1)} %convolution_bitcast_fusion.1), channel_id=1, source_target_pairs={{0,16},{16,0},{32,48},{48,32},{64,80},{80,64},{96,112},{112,96},{1... | collective-permute-start | bytes 32 | tf_op jit(solution)/shard_map/ppermute | solution.py:22
  37.2 48.1 %all-gather.2.cloned.1.call-done = bf16[1,9,512,512]{3,2,1,0:T(8,128)(2,1)} async-done(((bf16[1,9,32,512]{3,2,1,0:T(8,128)(2,1)}), bf16[1,9,512,512]{3,2,1,0:T(8,128)(2,1)}) %all-gather.2.cloned.1.call-update) | async-done | bytes 4718608 | tf_op jit(solution)/shard_map/all_gather | solution.py:131
  85.3 6.6 %copy.10 = bf16[9,512,512]{2,1,0:T(8,128)(2,1)} copy(bf16[9,512,512]{1,2,0:T(8,128)(2,1)} %bitcast.356) | data formatting | bytes 9437184 | tf_op jit(solution)/shard_map/transpose | solution.py:132
  92.0 5.1 %bitcast_abs_fusion = bf16[4608,512]{1,0:T(8,128)(2,1)} fusion(bf16[9,512,512]{2,1,0:T(8,128)(2,1)} %copy.10), kind=kLoop, calls=%fused_computation.517 | loop fusion | flops 2359296 | bytes 9437184 | tf_op jit(solution)/shard_map/abs | solution.py:133
  97.1 4.5 %conditional.10 = (f32[1,4,4,512]{3,2,1,0:T(4,128)S(1)}, f32[1,4,4,512]{3,2,1,0:T(4,128)S(1)}, f32[1,4,4,512]{3,2,1,0:T(4,128)S(1)}, f32[1,4,4,512]{3,2,1,0:T(4,128)S(1)}) conditional(s32[]{:T(128)} %convert_element_type.272, (f32[1,4,4,512]{3,2,1,0:T(4,128)S(1)}, f32[1,4,4,512]{3,2,1,0:T(4,128)S(1)}) %tuple.108, (f32[1,4,4,512]{3,2,1,0:T(4,128)S(1)}, ...), branch_computations={%region_2.3_spmd, %region_3.4_spmd} | conditional | flops 151175168 | bytes 10913824 | solution.py:157
  97.3 3.1 %fusion = f32[4,4,512]{2,1,0:T(4,128)S(1)} fusion(bf16[4608,512]{1,0:T(8,128)(2,1)} %get-tuple-element.592, bf16[1,4,4,4608]{3,2,1,0:T(4,128)(2,1)S(1)} %constant_dynamic-update-slice_fusion.9), kind=kOutput, calls=%fused_computation | convolution fusion | flops 75497472 | bytes 4898816 | tf_op jit(solution)/shard_map/cond/branch_1_fun/dot_general | solution.py:45
  101.6 1.3 collective-permute-start.4
  105.1 4.9 %conditional.11 = (f32[1,4,4,512]{3,2,1,0:T(4,128)S(1)}, f32[1,4,4,512]{3,2,1,0:T(4,128)S(1)}, f32[1,4,4,512]{3,2,1,0:T(4,128)S(1)}, f32[1,4,4,512]{3,2,1,0:T(4,128)S(1)}) conditional(s32[]{:T(128)} %convert_element_type.273, (f32[1,4,4,512]{3,2,1,0:T(4,128)S(1)}, f32[1,4,4,512]{3,2,1,0:T(4,128)S(1)}) %tuple.110, (f32[1,4,4,512]{3,2,1,0:T(4,128)S(1)}, ...), branch_computations={%region_4.5_spmd, %region_5.6_spmd} | conditional | flops 151175168 | bytes 29788220 | solution.py:157
  105.3 3.3 %fusion.9 = f32[4,4,512]{2,1,0:T(4,128)S(1)} fusion(bf16[4608,512]{1,0:T(8,128)(2,1)} %get-tuple-element.599, bf16[1,4,4,4608]{3,2,1,0:T(4,128)(2,1)S(1)} %constant_dynamic-update-slice_fusion.27), kind=kOutput, calls=%fused_computation.47 | convolution fusion | flops 75497472 | bytes 4898816 | tf_op jit(solution)/shard_map/cond/branch_1_fun/dot_general | solution.py:45
  110.0 3.6 %collective-permute-start.6 = (bf16[1,4,4,512]{3,2,1,0:T(4,128)(2,1)S(1)}, bf16[1,4,4,512]{3,2,1,0:T(4,128)(2,1)S(1)}, u32[]{:S(2)}, u32[]{:S(2)}) collective-permute-start(bf16[1,4,4,512]{3,2,1,0:T(4,128)(2,1)S(1)} %convert_element_type.281), channel_id=1, source_target_pairs={{0,128},{128,256},{256,384},{1,129},{129,257},{257,385},{2,130},{1... | collective-permute-start | bytes 49160 | tf_op jit(solution)/shard_map/ppermute | solution.py:16
  113.6 1.9 collective-permute-start.5
  116.5 8.5 %collective-permute-start.8 = (bf16[1,4,4,512]{3,2,1,0:T(4,128)(2,1)S(1)}, bf16[1,4,4,512]{3,2,1,0:T(4,128)(2,1)S(1)}, u32[]{:S(2)}, u32[]{:S(2)}) collective-permute-start(bf16[1,4,4,512]{3,2,1,0:T(4,128)(2,1)S(1)} %convert_element_type.286), channel_id=1, source_target_pairs={{0,128},{128,256},{256,384},{1,129},{129,257},{257,385},{2,130},{1... | collective-permute-start | bytes 49160 | tf_op jit(solution)/shard_map/ppermute | solution.py:16
  125.0 1.9 collective-permute-start.7
  127.9 3.6 %collective-permute-start.10 = (bf16[1,4,4,512]{3,2,1,0:T(4,128)(2,1)S(1)}, bf16[1,4,4,512]{3,2,1,0:T(4,128)(2,1)S(1)}, u32[]{:S(2)}, u32[]{:S(2)}) collective-permute-start(bf16[1,4,4,512]{3,2,1,0:T(4,128)(2,1)S(1)} %convert_element_type.291), channel_id=1, source_target_pairs={{0,128},{128,256},{256,384},{1,129},{129,257},{257,385},{2,130},{1... | collective-permute-start | bytes 49160 | tf_op jit(solution)/shard_map/ppermute | solution.py:16
  131.5 6.8 %collective-permute-start.9 = (bf16[1,4,4,512]{3,2,1,0:T(4,128)(2,1)S(1)}, bf16[1,4,4,512]{3,2,1,0:T(4,128)(2,1)S(1)}, u32[]{:S(2)}, u32[]{:S(2)}) collective-permute-start(bf16[1,4,4,512]{3,2,1,0:T(4,128)(2,1)S(1)} %convert_element_type.289), channel_id=1, source_target_pairs={{0,128},{128,256},{256,384},{1,129},{129,257},{257,385},{2,130},{1... | collective-permute-start | bytes 49160 | tf_op jit(solution)/shard_map/ppermute | solution.py:16
  139.5 1.3 collective-permute-start.11
  140.9 4.6 %collective-permute-done.11 = bf16[1,5,4,4,512]{4,1,3,2,0:T(8,128)(2,1)S(1)} collective-permute-done((bf16[1,5,4,4,512]{4,1,3,2,0:T(8,128)(2,1)S(1)}, bf16[1,5,4,4,512]{4,1,3,2,0:T(8,128)(2,1)S(1)}, u32[]{:S(2)}, u32[]{:S(2)}) %collective-permute-start.11) | collective-permute-done | bytes 81952 | tf_op jit(solution)/shard_map/ppermute | solution.py:16
  145.6 1.3 collective-permute-start.12
  146.9 4.6 %collective-permute-done.12 = bf16[1,5,4,4,512]{4,1,3,2,0:T(8,128)(2,1)S(1)} collective-permute-done((bf16[1,5,4,4,512]{4,1,3,2,0:T(8,128)(2,1)S(1)}, bf16[1,5,4,4,512]{4,1,3,2,0:T(8,128)(2,1)S(1)}, u32[]{:S(2)}, u32[]{:S(2)}) %collective-permute-start.12) | collective-permute-done | bytes 81952 | tf_op jit(solution)/shard_map/ppermute | solution.py:16
  151.7 1.3 collective-permute-start.13
  153.0 18.7 %collective-permute-done.13 = bf16[1,5,4,4,512]{4,1,3,2,0:T(8,128)(2,1)S(1)} collective-permute-done((bf16[1,5,4,4,512]{4,1,3,2,0:T(8,128)(2,1)S(1)}, bf16[1,5,4,4,512]{4,1,3,2,0:T(8,128)(2,1)S(1)}, u32[]{:S(2)}, u32[]{:S(2)}) %collective-permute-start.13) | collective-permute-done | bytes 81952 | tf_op jit(solution)/shard_map/ppermute | solution.py:16
  171.7 4.4 %conditional.18 = (f32[1,5,4,4,512]{4,1,3,2,0:T(8,128)S(1)}, f32[1,5]{1,0:T(1,128)S(1)}) conditional(s32[]{:T(128)} %convert_element_type.303, f32[1,5,4,4,512]{4,1,3,2,0:T(8,128)S(1)} %convert_select_fusion, (f32[2,4,4,512]{3,2,1,0:T(4,128)S(1)}, s32[]{:T(128)}, f32[1,5,4,4,512]{4,1,3,2,0:T(8,128)S(1)}, bf16[4608,512]{1,0:T(8,128)(2,1)}, ...), branch_computations={%region_24.25_spmd, %region_25.28_spmd} | conditional | flops 378019872 | bytes 8734866 | solution.py:207
  172.2 3.9 %subtract_reduce_fusion.3 = (f32[5]{0:T(128)S(1)}, f32[1,5,4,4,512]{4,1,3,2,0:T(8,128)S(1)}) fusion(f32[4,4,512]{2,1,0:T(4,128)S(1)} %get-tuple-element.776, f32[4,4,512]{2,1,0:T(4,128)S(1)} %get-tuple-element.777, f32[1,5,4,4,512]{4,1,3,2,0:T(8,128)S(1)} %get-tuple-element.656, bf16[5,4,4,4608]{3,0,2,1:T(8,128)(2,1)S(1)} %fusion.122, ...), kind=kOutput, calls=%fused_computation.349 | convolution fusion | flops 377733120 | bytes 5849108 | tf_op jit(solution)/shard_map/cond/branch_1_fun/dot_general | solution.py:62
  176.2 1.3 collective-permute-start.14
  177.5 4.4 %collective-permute-done.14 = bf16[1,5,4,4,512]{4,1,3,2,0:T(8,128)(2,1)S(1)} collective-permute-done((bf16[1,5,4,4,512]{4,1,3,2,0:T(8,128)(2,1)S(1)}, bf16[1,5,4,4,512]{4,1,3,2,0:T(8,128)(2,1)S(1)}, u32[]{:S(2)}, u32[]{:S(2)}) %collective-permute-start.14) | collective-permute-done | bytes 81952 | tf_op jit(solution)/shard_map/ppermute | solution.py:16
  182.0 4.4 %conditional.19 = (f32[1,5]{1,0:T(1,128)S(1)}) conditional(s32[]{:T(128)} %convert_element_type.308, () %tuple.122, (f32[5,512]{1,0:T(8,128)S(1)}, pred[1,5,4,4,512]{4,1,3,2,0:T(8,128)(4,1)S(1)}, f32[1,5,4,4,512]{4,1,3,2,0:T(8,128)S(1)}, f32[2,4,4,512]{3,2,1,0:T(4,128)S(1)}, s32[]{:T(128)}, /*index=5*/f32[1,512]{1,0:T(1,128)S(1)}, ...), branch_computations={%region_28.29_spmd, %region_29.32_spmd} | conditional | flops 378104352 | bytes 8693898 | solution.py:207
  182.5 3.9 %subtract_reduce_fusion.4 = f32[5]{0:T(128)S(1)} fusion(bf16[5,4,4,4608]{3,0,2,1:T(8,128)(2,1)S(1)} %fusion.144, bf16[4608,512]{1,0:T(8,128)(2,1)} %get-tuple-element.677, f32[4,4,512]{2,1,0:T(4,128)S(1)} %get-tuple-element.782, f32[4,4,512]{2,1,0:T(4,128)S(1)} %get-tuple-element.783, pred[1,5,4,4,512]{4,1,3,2,0:T(8,128)(4,1)S(1)} %get-tuple-element.667, ...), kind=kOutput, calls=%fused_computation.383 | convolution fusion | flops 377774080 | bytes 5736468 | tf_op jit(solution)/shard_map/cond/branch_1_fun/dot_general | solution.py:62
  186.8 18.7 %collective-permute-start.15 = (f32[2,5]{1,0:T(2,128)S(1)}, f32[2,5]{1,0:T(2,128)S(1)}, u32[]{:S(2)}, u32[]{:S(2)}) collective-permute-start(f32[2,5]{1,0:T(2,128)S(1)} %fusion.174), channel_id=1, source_target_pairs={{0,16},{16,0},{32,48},{48,32},{64,80},{80,64},{96,112},{112,96},{1... | collective-permute-start | bytes 128 | tf_op jit(solution)/shard_map/ppermute | solution.py:22
  206.5 6.5 %all_to_all.5 = f32[4,1,5]{2,1,0:T(1,128)S(1)} all-to-all(f32[4,1,5]{2,1,0:T(1,128)S(1)} %bitcast.376), channel_id=1, replica_groups=mesh['segment'=4,'rep'=8,'box'=16] {'segment'}, dimensions={0} | all-to-all | bytes 160 | tf_op jit(solution)/shard_map/all_to_all | solution.py:33
  (207 shorter events, 24.0 us)
Async XLA Ops:
  6.5 28.8 %copy-start = (bf16[512,10]{0,1:T(8,128)(2,1)S(1)}, bf16[512,10]{0,1:T(8,128)(2,1)}, u32[]{:S(2)}) copy-start(bf16[512,10]{0,1:T(8,128)(2,1)} %param.34) | copy-start | bytes 30724
  6.5 16.8 %copy-start.7 = (s32[4]{0:T(128)S(1)}, s32[4]{0:T(128)}, u32[]{:S(2)}) copy-start(s32[4]{0:T(128)} %param.30) | copy-start | bytes 52
  6.5 27.9 %copy-start.8 = (f32[10]{0:T(128)S(1)}, f32[10]{0:T(128)}, u32[]{:S(2)}) copy-start(f32[10]{0:T(128)} %param.35) | copy-start | bytes 124
  6.5 78.8 %all-gather.2.cloned.1.call-start = ((), (), s32[]{:S(2)}) async-start(), calls=%async_computation.1 | async-start | bytes 5013504 | tf_op jit(solution)/shard_map/all_gather | solution.py:131
  11.4 25.1 %collective-permute-start.1 = (f32[2,8192]{1,0:T(2,128)S(1)}, f32[2,8192]{1,0:T(2,128)S(1)}, u32[]{:S(2)}, u32[]{:S(2)}) collective-permute-start(f32[2,8192]{1,0:T(2,128)S(1)} %fusion.194), channel_id=1, source_target_pairs={{0,16},{16,0},{32,48},{48,32},{64,80},{80,64},{96,112},{112,96},{1... | collective-permute-start | bytes 196616 | tf_op jit(solution)/shard_map/ppermute | solution.py:22
  21.4 15.4 %collective-permute-start.2 = (f32[2,8192]{1,0:T(2,128)S(1)}, f32[2,8192]{1,0:T(2,128)S(1)}, u32[]{:S(2)}, u32[]{:S(2)}) collective-permute-start(f32[2,8192]{1,0:T(2,128)S(1)} %fusion.196), channel_id=1, source_target_pairs={{0,16},{16,0},{32,48},{48,32},{64,80},{80,64},{96,112},{112,96},{1... | collective-permute-start | bytes 196616 | tf_op jit(solution)/shard_map/ppermute | solution.py:22
  23.5 3.8 %collective-permute-start = (f32[2,1]{0,1:T(1,128)S(1)}, f32[2,1]{0,1:T(1,128)S(1)}, u32[]{:S(2)}, u32[]{:S(2)}) collective-permute-start(f32[2,1]{0,1:T(1,128)S(1)} %convolution_bitcast_fusion.1), channel_id=1, source_target_pairs={{0,16},{16,0},{32,48},{48,32},{64,80},{80,64},{96,112},{112,96},{1... | collective-permute-start | bytes 32 | tf_op jit(solution)/shard_map/ppermute | solution.py:22
  92.0 5.1 %copy-start.1 = (bf16[9,512,512]{2,1,0:T(8,128)(2,1)S(1)}, bf16[9,512,512]{2,1,0:T(8,128)(2,1)}, u32[]{:S(2)}) copy-start(bf16[9,512,512]{2,1,0:T(8,128)(2,1)} %copy.10) | copy-start | bytes 14155780
  92.0 5.1 %copy-start.6 = (f32[1,512]{1,0:T(1,128)S(1)}, f32[1,512]{1,0:T(1,128)}, u32[]{:S(2)}) copy-start(f32[1,512]{1,0:T(1,128)} %param.33) | copy-start | bytes 6148
  101.6 2.7 %collective-permute-start.4 = (bf16[1,4,4,512]{3,2,1,0:T(4,128)(2,1)S(1)}, bf16[1,4,4,512]{3,2,1,0:T(4,128)(2,1)S(1)}, u32[]{:S(2)}, u32[]{:S(2)}) collective-permute-start(bf16[1,4,4,512]{3,2,1,0:T(4,128)(2,1)S(1)} %convert_element_type.276), channel_id=1, source_target_pairs={{0,128},{128,256},{256,384},{1,129},{129,257},{257,385},{2,130},{1... | collective-permute-start | bytes 49160 | tf_op jit(solution)/shard_map/ppermute | solution.py:16
  102.9 2.1 collective-permute-start.3
  105.3 3.8 %copy-start.2 = (bf16[4608,512]{1,0:T(8,128)(2,1)S(1)}, bf16[4608,512]{1,0:T(8,128)(2,1)}, u32[]{:S(2)}) copy-start(bf16[4608,512]{1,0:T(8,128)(2,1)} %get-tuple-element.596) | copy-start | bytes 14155780 | tf_op jit(solution)/shard_map/cond
  110.0 5.6 %collective-permute-start.6 = (bf16[1,4,4,512]{3,2,1,0:T(4,128)(2,1)S(1)}, bf16[1,4,4,512]{3,2,1,0:T(4,128)(2,1)S(1)}, u32[]{:S(2)}, u32[]{:S(2)}) collective-permute-start(bf16[1,4,4,512]{3,2,1,0:T(4,128)(2,1)S(1)} %convert_element_type.281), channel_id=1, source_target_pairs={{0,128},{128,256},{256,384},{1,129},{129,257},{257,385},{2,130},{1... | collective-permute-start | bytes 49160 | tf_op jit(solution)/shard_map/ppermute | solution.py:16
  113.6 2.8 %collective-permute-start.5 = (bf16[1,4,4,512]{3,2,1,0:T(4,128)(2,1)S(1)}, bf16[1,4,4,512]{3,2,1,0:T(4,128)(2,1)S(1)}, u32[]{:S(2)}, u32[]{:S(2)}) collective-permute-start(bf16[1,4,4,512]{3,2,1,0:T(4,128)(2,1)S(1)} %convert_element_type.279), channel_id=1, source_target_pairs={{0,128},{128,256},{256,384},{1,129},{129,257},{257,385},{2,130},{1... | collective-permute-start | bytes 49160 | tf_op jit(solution)/shard_map/ppermute | solution.py:16
  116.5 10.5 %collective-permute-start.8 = (bf16[1,4,4,512]{3,2,1,0:T(4,128)(2,1)S(1)}, bf16[1,4,4,512]{3,2,1,0:T(4,128)(2,1)S(1)}, u32[]{:S(2)}, u32[]{:S(2)}) collective-permute-start(bf16[1,4,4,512]{3,2,1,0:T(4,128)(2,1)S(1)} %convert_element_type.286), channel_id=1, source_target_pairs={{0,128},{128,256},{256,384},{1,129},{129,257},{257,385},{2,130},{1... | collective-permute-start | bytes 49160 | tf_op jit(solution)/shard_map/ppermute | solution.py:16
  125.0 2.8 %collective-permute-start.7 = (bf16[1,4,4,512]{3,2,1,0:T(4,128)(2,1)S(1)}, bf16[1,4,4,512]{3,2,1,0:T(4,128)(2,1)S(1)}, u32[]{:S(2)}, u32[]{:S(2)}) collective-permute-start(bf16[1,4,4,512]{3,2,1,0:T(4,128)(2,1)S(1)} %convert_element_type.284), channel_id=1, source_target_pairs={{0,128},{128,256},{256,384},{1,129},{129,257},{257,385},{2,130},{1... | collective-permute-start | bytes 49160 | tf_op jit(solution)/shard_map/ppermute | solution.py:16
  127.9 10.5 %collective-permute-start.10 = (bf16[1,4,4,512]{3,2,1,0:T(4,128)(2,1)S(1)}, bf16[1,4,4,512]{3,2,1,0:T(4,128)(2,1)S(1)}, u32[]{:S(2)}, u32[]{:S(2)}) collective-permute-start(bf16[1,4,4,512]{3,2,1,0:T(4,128)(2,1)S(1)} %convert_element_type.291), channel_id=1, source_target_pairs={{0,128},{128,256},{256,384},{1,129},{129,257},{257,385},{2,130},{1... | collective-permute-start | bytes 49160 | tf_op jit(solution)/shard_map/ppermute | solution.py:16
  131.5 7.6 %collective-permute-start.9 = (bf16[1,4,4,512]{3,2,1,0:T(4,128)(2,1)S(1)}, bf16[1,4,4,512]{3,2,1,0:T(4,128)(2,1)S(1)}, u32[]{:S(2)}, u32[]{:S(2)}) collective-permute-start(bf16[1,4,4,512]{3,2,1,0:T(4,128)(2,1)S(1)} %convert_element_type.289), channel_id=1, source_target_pairs={{0,128},{128,256},{256,384},{1,129},{129,257},{257,385},{2,130},{1... | collective-permute-start | bytes 49160 | tf_op jit(solution)/shard_map/ppermute | solution.py:16
  139.5 6.0 %collective-permute-start.11 = (bf16[1,5,4,4,512]{4,1,3,2,0:T(8,128)(2,1)S(1)}, bf16[1,5,4,4,512]{4,1,3,2,0:T(8,128)(2,1)S(1)}, u32[]{:S(2)}, u32[]{:S(2)}) collective-permute-start(bf16[1,5,4,4,512]{4,1,3,2,0:T(8,128)(2,1)S(1)} %convert_element_type.296), channel_id=1, source_target_pairs={{128,0},{256,128},{384,256},{129,1},{257,129},{385,257},{130,2},{2... | collective-permute-start | bytes 245768 | tf_op jit(solution)/shard_map/ppermute | solution.py:16
  145.6 6.0 %collective-permute-start.12 = (bf16[1,5,4,4,512]{4,1,3,2,0:T(8,128)(2,1)S(1)}, bf16[1,5,4,4,512]{4,1,3,2,0:T(8,128)(2,1)S(1)}, u32[]{:S(2)}, u32[]{:S(2)}) collective-permute-start(bf16[1,5,4,4,512]{4,1,3,2,0:T(8,128)(2,1)S(1)} %convert_element_type.301), channel_id=1, source_target_pairs={{128,0},{256,128},{384,256},{129,1},{257,129},{385,257},{130,2},{2... | collective-permute-start | bytes 245768 | tf_op jit(solution)/shard_map/ppermute | solution.py:16
  151.7 20.0 %collective-permute-start.13 = (bf16[1,5,4,4,512]{4,1,3,2,0:T(8,128)(2,1)S(1)}, bf16[1,5,4,4,512]{4,1,3,2,0:T(8,128)(2,1)S(1)}, u32[]{:S(2)}, u32[]{:S(2)}) collective-permute-start(bf16[1,5,4,4,512]{4,1,3,2,0:T(8,128)(2,1)S(1)} %convert_element_type.306), channel_id=1, source_target_pairs={{128,0},{256,128},{384,256},{129,1},{257,129},{385,257},{130,2},{2... | collective-permute-start | bytes 245768 | tf_op jit(solution)/shard_map/ppermute | solution.py:16
  176.2 5.7 %collective-permute-start.14 = (bf16[1,5,4,4,512]{4,1,3,2,0:T(8,128)(2,1)S(1)}, bf16[1,5,4,4,512]{4,1,3,2,0:T(8,128)(2,1)S(1)}, u32[]{:S(2)}, u32[]{:S(2)}) collective-permute-start(bf16[1,5,4,4,512]{4,1,3,2,0:T(8,128)(2,1)S(1)} %convert_element_type.311), channel_id=1, source_target_pairs={{128,0},{256,128},{384,256},{129,1},{257,129},{385,257},{130,2},{2... | collective-permute-start | bytes 245768 | tf_op jit(solution)/shard_map/ppermute | solution.py:16
  186.8 19.5 %collective-permute-start.15 = (f32[2,5]{1,0:T(2,128)S(1)}, f32[2,5]{1,0:T(2,128)S(1)}, u32[]{:S(2)}, u32[]{:S(2)}) collective-permute-start(f32[2,5]{1,0:T(2,128)S(1)} %fusion.174), channel_id=1, source_target_pairs={{0,16},{16,0},{32,48},{48,32},{64,80},{80,64},{96,112},{112,96},{1... | collective-permute-start | bytes 128 | tf_op jit(solution)/shard_map/ppermute | solution.py:22
Sparse Core Ops, SparseCore 0:
  9.4 75.8 all-gather.1
where the time goes:
time: 221 us; the launch traced here: 220 us
  waiting for transfers between devices  85 us (38%)
  starting transfers between devices  65.8 us (30%)
  matrix products  20.2 us (9%)
  between operations  17.3 us (8%)
  other arithmetic  13.7 us (6%)
  local copies, waits for them, and re-layouts  11.1 us (5%)
  blocking collectives  6.47 us (3%)
    all_gather x1, waiting for transfers between devices, run_sections(): kernel = lax.all_gather(conv_weights, 'box', axis=2, tiled=True)[0]  48.1 us
    ppermute x12, waiting for transfers between devices, shifted(): return lax.ppermute(x, axis, pairs)  35.3 us
    ppermute x12, starting transfers between devices, shifted(): return lax.ppermute(x, axis, pairs)  34.1 us
    ppermute x4, starting transfers between devices, partner(): return lax.ppermute(value, axis, pairs)  31.7 us
    dot_general x4, matrix products, convolve(): lax.dot_general(stacked, kernel_cols, (((3,), (0,)), ((), ())), preferred...  7.97 us
    dot_general x2, matrix products, convolve_back(): lax.dot_general(stacked, kernel_rows, (((3,), (0,)), ((), ())), preferred...  7.83 us
    transpose x1, local copies, waits for them, and re-layouts, run_sections(): jnp.transpose(kernel, (0, 2, 1)).reshape(9 * channels, channels)  6.65 us
    all_to_all x1, blocking collectives, summed_on_arrival(): parts = lax.all_to_all(in_blocks(x, dim, count), axis, 0, 0, tiled=True)  6.47 us
  transfers between devices with their start and end apart: 17, of which 10 were waited for; matrix products, arithmetic and copies ran while one was open for 6% of the time, Pallas kernels for 0%

commit v1 on v0

v1 whole, which is shorter than its diff:
```python
import functools

import jax
import jax.numpy as jnp
from jax import lax
from jax.experimental import pallas as pl
from jax.experimental.pallas import tpu as pltpu
from jax.sharding import PartitionSpec as P

K = 5
CHUNKS = 3
TAPS = 9
bf16 = jnp.bfloat16
f32 = jnp.float32
MESH = pl.DeviceIdType.MESH


def kernel(
    n_seg, n_rep, n_box, classes,
    cert, lab, cen, rad, cw, bias, hw, hb, out,
    W, S, L, G, C8, R8, PT, MID, fin, fout, cin, cout, CF, slope, cept, HC, HO, T,
    loc, zs, zr, ys, yr, cs, cr, xs, xr, fs, fr, bs, br, ts, tr,
):
    s = lax.axis_index("segment")
    r = lax.axis_index("rep")
    z = lax.axis_index("box")
    c = lax.rem(r, 2)
    par = lax.rem(r // 2, 2)
    mate = {"rep": r + 1 - 2 * c}
    y_up = {"rep": lax.rem(r + 2, n_rep)}
    y_down = {"rep": lax.rem(r + n_rep - 2, n_rep)}
    z_up = {"box": lax.rem(z + 1, n_box)}
    z_down = {"box": lax.rem(z + n_box - 1, n_box)}
    peers = []
    for dx in range(n_seg):
        for dc in range(2):
            if dx or dc:
                peers.append(
                    {"segment": lax.rem(s + dx, n_seg), "rep": r + dc * (1 - 2 * c)}
                )
    shard = W.shape[1] // n_box
    half = shard // 2
    lanes = W.shape[2] // 2
    per = TAPS // CHUNKS
    last_up = n_box // 2
    last_down = n_box - 1 - last_up

    own = pltpu.make_async_copy(
        cw.at[0], W.at[:, pl.ds(pl.multiple_of(z * shard, shard), shard), :], loc.at[0]
    )
    own.start()
    own_c = pltpu.make_async_copy(cen, C8.at[pl.ds(4 * c, 4)], loc.at[1])
    own_c.start()
    own_r = pltpu.make_async_copy(rad, R8.at[pl.ds(4 * c, 4)], loc.at[2])
    own_r.start()

    barrier = pltpu.get_barrier_semaphore()
    near = [y_up, y_down, z_up, z_down] + peers
    for device in near:
        pl.semaphore_signal(barrier, inc=1, device_id=device, device_id_type=MESH)
    pl.semaphore_wait(barrier, len(near))

    def remote(src, dst, send, recv, device):
        return pltpu.make_async_remote_copy(
            src_ref=src, dst_ref=dst, send_sem=send, recv_sem=recv,
            device_id=device, device_id_type=MESH,
        )

    def piece(b, core, side, j=None):
        row = pl.multiple_of(b * shard + core * half, half)
        lane = pl.multiple_of(side * lanes, lanes)
        taps = pl.ds(0, TAPS) if j is None else pl.ds(j * per, per)
        return W.at[taps, pl.ds(row, half), pl.ds(lane, lanes)]

    def source(d, k):
        if d == 0:
            return lax.rem(z + n_box - k, n_box)
        return lax.rem(z + k, n_box)

    def z_copy(d, k, j):
        ref = piece(source(d, k - 1), c, par, j)
        return remote(ref, ref, zs.at[d, k - 1, j], zr.at[d, k - 1, j], (z_up, z_down)[d])

    def z_land(d, k, j):
        ref = piece(source(d, k), c, par, j)
        remote(ref, ref, zs.at[d, k - 1, j], zr.at[d, k - 1, j], (z_up, z_down)[d]).wait_recv()

    def y_copy(d, k, j):
        ref = piece(source(d, k), c, par, j)
        return remote(ref, ref, ys.at[d, k - 1, j], yr.at[d, k - 1, j], (y_up, y_down)[d])

    def y_land(d, k, j):
        ref = piece(source(d, k), c, 1 - par, j)
        remote(ref, ref, ys.at[d, k - 1, j], yr.at[d, k - 1, j], (y_up, y_down)[d]).wait_recv()

    def c_copy(d, k, h):
        ref = piece(source(d, k), c, par if h == 0 else 1 - par)
        return remote(ref, ref, cs.at[d, k - 1, h], cr.at[d, k - 1, h], mate)

    def c_land(d, k, h):
        ref = piece(source(d, k), 1 - c, par if h == 0 else 1 - par)
        remote(ref, ref, cs.at[d, k - 1, h], cr.at[d, k - 1, h], mate).wait_recv()

    own.wait()
    for j in range(CHUNKS):
        z_copy(0, 1, j).start()
        z_copy(1, 1, j).start()

    own_c.wait()
    own_r.wait()
    pair_c = remote(C8.at[pl.ds(4 * c, 4)], C8.at[pl.ds(4 * c, 4)], xs.at[0], xr.at[0], mate)
    pair_r = remote(R8.at[pl.ds(4 * c, 4)], R8.at[pl.ds(4 * c, 4)], xs.at[1], xr.at[1], mate)
    row8 = lax.broadcasted_iota(jnp.int32, (8, 128), 0)
    lane8 = lax.broadcasted_iota(jnp.int32, (8, 128), 1)
    tile = jnp.zeros((8, 128), f32)
    for i in range(4):
        alive_i = (1 - cert[i]).astype(f32)
        label_i = lab[i].astype(f32)
        here = lane8 == 4 * c + i
        tile = jnp.where(here & (row8 == 0), alive_i, tile)
        tile = jnp.where(here & (row8 == 1), label_i, tile)
    PT[c] = tile
    pair_t = remote(PT.at[c], PT.at[c], xs.at[2], xr.at[2], mate)
    pair_t.start()
    pair_c.start()
    pair_r.start()

    p_row = lax.broadcasted_iota(jnp.int32, (80, 128), 0)
    p_col = lax.broadcasted_iota(jnp.int32, (80, 128), 1)
    same = (p_row // 16) == (p_col // 16)
    dy = lax.rem(p_col, 16) // 4 - lax.rem(p_row, 16) // 4
    dx_ = lax.rem(p_col, 4) - lax.rem(p_row, 4)
    for t in range(TAPS):
        a, b = divmod(t, 3)
        S[t] = jnp.where(same & (dy == a - 1) & (dx_ == b - 1), 1.0, 0.0).astype(bf16)
    G[...] = jnp.zeros_like(G)

    def gather_step(k, _):
        for d in range(2):
            for j in range(CHUNKS):
                z_land(d, k, j)
                go_on = k < (last_up, last_down)[d]

                @pl.when(go_on)
                def _():
                    z_copy(d, k + 1, j).start()

                y_copy(d, k, j).start()
            c_copy(d, k, 0).start()

        @pl.when(k > 1)
        def _():
            for d in range(2):
                for j in range(CHUNKS):
                    y_land(d, k - 1, j)
                c_copy(d, k - 1, 1).start()

        return 0

    lax.fori_loop(1, last_down + 1, gather_step, 0)
    if last_up > last_down:
        for j in range(CHUNKS):
            z_land(0, last_up, j)
            y_copy(0, last_up, j).start()
        c_copy(0, last_up, 0).start()
    for d in range(2):
        for j in range(CHUNKS):
            y_land(d, last_down, j)
        c_copy(d, last_down, 1).start()
    if last_up > last_down:
        for j in range(CHUNKS):
            y_land(0, last_up, j)
        c_copy(0, last_up, 1).start()

    remote(PT.at[1 - c], PT.at[1 - c], xs.at[2], xr.at[2], mate).wait_recv()
    other = pl.ds(4 * (1 - c), 4)
    remote(C8.at[other], C8.at[other], xs.at[0], xr.at[0], mate).wait_recv()
    remote(R8.at[other], R8.at[other], xs.at[1], xr.at[1], mate).wait_recv()
    both = PT[0] + PT[1]
    alive_row = both[0:1, :]
    label_row = both[1:2, :]
    alive = jnp.sum(jnp.where(lane8 == row8, alive_row, 0.0), axis=1, keepdims=True)
    labels = jnp.sum(jnp.where(lane8 == row8, label_row, 0.0), axis=1, keepdims=True)
    rank = jnp.sum(jnp.where(lane8 < row8, alive_row, 0.0), axis=1, keepdims=True)
    live_no = jnp.where(alive > 0.5, rank, -1.0)
    first = (2 * c).astype(f32)

    @pl.when(s == 0)
    def _():
        for m in range(2):
            pick = jnp.where(live_no == first + m, 1.0, 0.0)
            middle = jnp.zeros((16, C8.shape[3]), f32)
            radius = jnp.zeros((16, C8.shape[3]), f32)
            for i in range(8):
                take = pick[i : i + 1, :] > 0.5
                middle = jnp.where(take, C8[i].reshape(middle.shape), middle)
                radius = jnp.where(take, R8[i].reshape(radius.shape), radius)
            MID[16 * m : 16 * m + 16] = middle
            MID[32 + 16 * m : 48 + 16 * m] = radius

    @pl.when(s == n_seg - 1)
    def _():
        row = lax.broadcasted_iota(jnp.int32, (16, 1), 0)
        spec = lax.rem(row, 8).astype(f32)
        lab0 = jnp.sum(jnp.where(live_no == first, labels, 0.0), axis=0, keepdims=True)
        lab1 = jnp.sum(jnp.where(live_no == first + 1.0, labels, 0.0), axis=0, keepdims=True)
        true = jnp.where(row < 8, lab0, lab1)
        rival = true + 1.0 + spec
        rival = jnp.where(rival >= classes, rival - classes, rival)
        ids = lax.broadcasted_iota(jnp.int32, (16, classes), 1).astype(f32)
        selector = jnp.where(ids == true, 1.0, 0.0) - jnp.where(ids == rival, 1.0, 0.0)
        selector = jnp.where(spec < K, selector, 0.0)
        pooled = lax.dot_general(
            selector.astype(bf16), hw[...], (((1,), (1,)), ((), ())), preferred_element_type=f32
        ) / 16.0
        HC[...] = pooled.reshape(2, 8, pooled.shape[1])
        offset = jnp.sum(selector * hb[...], axis=1, keepdims=True)
        lane16 = lax.broadcasted_iota(jnp.int32, (16, 128), 1)
        HO[...] = jnp.where(lane16 == 0, offset, 0.0)

    for d in range(2):
        for k in range(1, (last_up, last_down)[d] + 1):
            for h in range(2):
                c_land(d, k, h)

    @pl.when(s > 0)
    def _():
        remote(fout, fin, fs, fr, {"segment": lax.rem(s + 1, n_seg)}).wait_recv()
        MID[...] = fin[...].astype(f32)

    G[0:64] = MID[...].astype(bf16)
    for t in range(TAPS):
        L[t, 0:64] = jnp.dot(
            S[t, 0:64], G[...], preferred_element_type=f32
        ).astype(bf16)
    rows_in = (((1,), (1,)), ((), ()))
    centre = jnp.zeros((32, W.shape[1]), f32)
    spread = jnp.zeros((32, W.shape[1]), f32)
    for t in range(TAPS):
        w = W[t]
        centre += lax.dot_general(L[t, 0:32], w, rows_in, preferred_element_type=f32)
        spread += lax.dot_general(
            L[t, 32:64], jnp.abs(w), rows_in, preferred_element_type=f32
        )
    centre = centre + bias[...]
    low = centre - spread
    up = centre + spread
    up_pos = jnp.maximum(up, 0.0)
    low_pos = jnp.maximum(low, 0.0)
    low_neg = jnp.maximum(-low, 0.0)
    fout[0:32] = (MID[0:32] + 0.5 * (up_pos + low_pos)).astype(bf16)
    fout[32:64] = (MID[32:64] + 0.5 * (up_pos - low_pos)).astype(bf16)

    @pl.when(s < n_seg - 1)
    def _():
        remote(fout, fin, fs, fr, {"segment": lax.rem(s + 1, n_seg)}).start()

    slope_now = up_pos / (up_pos + low_neg)
    cept_now = slope_now * low_neg
    slope[...] = slope_now.reshape(slope.shape)
    cept[...] = cept_now.reshape(cept.shape)

    slot = s * 2 + c
    down_x = {"segment": lax.rem(s + n_seg - 1, n_seg)}
    for m in range(2):
        @pl.when(s == n_seg - 1)
        def _():
            for k in range(K):
                CF[16 * k : 16 * k + 16] = jnp.broadcast_to(
                    HC[m, k : k + 1], (16, HC.shape[2])
                )

        @pl.when(s < n_seg - 1)
        def _():
            remote(cout.at[m], cin.at[m], bs.at[m], br.at[m], down_x).wait_recv()
            CF[...] = cin[m].astype(f32)

        slope_m = slope[m]
        for k in range(K):
            G[16 * k : 16 * k + 16] = (CF[16 * k : 16 * k + 16] * slope_m).astype(bf16)
        for t in range(TAPS):
            L[t] = jnp.dot(S[TAPS - 1 - t], G[...], preferred_element_type=f32).astype(bf16)
        new = CF[...]
        for t in range(TAPS):
            new += jnp.dot(L[t], W[t], preferred_element_type=f32)

        @pl.when(s > 0)
        def _():
            cout[m] = new.astype(bf16)
            remote(cout.at[m], cin.at[m], bs.at[m], br.at[m], down_x).start()

        cept_m = cept[m]
        first_section = s == 0
        for k in range(K):
            now = CF[16 * k : 16 * k + 16]
            part = now * slope_m * bias[...] + jnp.minimum(now, 0.0) * cept_m
            new_k = new[16 * k : 16 * k + 16]
            ends = new_k * MID[16 * m : 16 * m + 16] - jnp.abs(new_k) * MID[
                32 + 16 * m : 48 + 16 * m
            ]
            part = part + jnp.where(first_section, ends, 0.0)
            part = jnp.sum(part, axis=0, keepdims=True)
            folded = part[:, 0:128]
            for q in range(1, part.shape[1] // 128):
                folded = folded + part[:, 128 * q : 128 * q + 128]
            at = 8 * m + k
            folded = folded + jnp.where(s == n_seg - 1, HO[at : at + 1, :], 0.0)
            T[slot, at : at + 1, :] = folded

    sends = []
    for n, device in enumerate(peers):
        copy = remote(T.at[slot], T.at[slot], ts.at[n], tr.at[slot], device)
        copy.start()
        sends.append(copy)
    for dx in range(n_seg):
        for dc in range(2):
            if dx or dc:
                there = lax.rem(s + dx, n_seg) * 2 + c + dc * (1 - 2 * c)
                remote(T.at[there], T.at[there], ts.at[0], tr.at[there], mate).wait_recv()
    mine = jnp.where(row8[:, 0:1] == 4 * c + s, live_no, -1.0)
    mine = jnp.max(mine, axis=0, keepdims=True)
    total = jnp.zeros((8, 128), f32)
    for core in range(2):
        for m in range(2):
            part = T[core, 8 * m : 8 * m + 8]
            for x in range(1, n_seg):
                part = part + T[2 * x + core, 8 * m : 8 * m + 8]
            total = jnp.where((mine == float(2 * core + m)) & (row8 < K), part, total)
    column = jnp.sum(total, axis=1, keepdims=True)
    line = jnp.sum(jnp.where(row8 == lane8, column, 0.0), axis=0, keepdims=True)
    out[0] = line[:, 0:K]

    for copy in sends:
        copy.wait_send()

    def drain(k, _):
        for d in range(2):
            for j in range(CHUNKS):
                z_copy(d, k, j).wait_send()
                y_copy(d, k, j).wait_send()
            for h in range(2):
                c_copy(d, k, h).wait_send()
        return 0

    lax.fori_loop(1, last_down + 1, drain, 0)
    if last_up > last_down:
        for j in range(CHUNKS):
            z_copy(0, last_up, j).wait_send()
            y_copy(0, last_up, j).wait_send()
        for h in range(2):
            c_copy(0, last_up, h).wait_send()
    pair_c.wait_send()
    pair_r.wait_send()
    pair_t.wait_send()

    @pl.when(s < n_seg - 1)
    def _():
        remote(fout, fin, fs, fr, {"segment": lax.rem(s + 1, n_seg)}).wait_send()

    @pl.when(s > 0)
    def _():
        for m in range(2):
            remote(cout.at[m], cin.at[m], bs.at[m], br.at[m], down_x).wait_send()


def per_device(mesh_shape, centers, box_radii, labels, certified, conv_weights, conv_bias,
               head_weight, head_bias):
    n_seg, n_rep, n_box = (mesh_shape[a] for a in ("segment", "rep", "box"))
    h = conv_weights.shape[-1]
    classes = head_bias.shape[0]
    steps = n_box // 2
    dma = pltpu.SemaphoreType.DMA
    vmem = pl.BlockSpec(memory_space=pltpu.VMEM)
    smem = pl.BlockSpec(memory_space=pltpu.SMEM)
    hbm = pl.BlockSpec(memory_space=pl.ANY)
    return pl.pallas_call(
        functools.partial(kernel, n_seg, n_rep, n_box, classes),
        out_shape=jax.ShapeDtypeStruct((1, 1, K), f32),
        in_specs=[smem, smem, hbm, hbm, hbm, vmem, vmem, vmem],
        out_specs=vmem,
        scratch_shapes=[
            pltpu.VMEM((TAPS, h, h), bf16),
            pltpu.VMEM((TAPS, 80, 128), bf16),
            pltpu.VMEM((TAPS, 80, h), bf16),
            pltpu.VMEM((128, h), bf16),
            pltpu.VMEM((8, 4, 4, h), f32),
            pltpu.VMEM((8, 4, 4, h), f32),
            pltpu.VMEM((2, 8, 128), f32),
            pltpu.VMEM((64, h), f32),
            pltpu.VMEM((64, h), bf16),
            pltpu.VMEM((64, h), bf16),
            pltpu.VMEM((2, 80, h), bf16),
            pltpu.VMEM((2, 80, h), bf16),
            pltpu.VMEM((80, h), f32),
            pltpu.VMEM((2, 16, h), f32),
            pltpu.VMEM((2, 16, h), f32),
            pltpu.VMEM((2, 8, h), f32),
            pltpu.VMEM((16, 128), f32),
            pltpu.VMEM((2 * n_seg, 16, 128), f32),
            dma((3,)),
            dma((2, steps, CHUNKS)),
            dma((2, steps, CHUNKS)),
            dma((2, steps, CHUNKS)),
            dma((2, steps, CHUNKS)),
            dma((2, steps, 2)),
            dma((2, steps, 2)),
            dma((3,)),
            dma((3,)),
            dma,
            dma,
            dma((2,)),
            dma((2,)),
            dma((2 * n_seg,)),
            dma((2 * n_seg,)),
        ],
        compiler_params=pltpu.CompilerParams(collective_id=0, has_side_effects=True),
    )(certified, labels, centers, box_radii, conv_weights, conv_bias, head_weight,
      head_bias[None, :])


def solution(mesh):
    placed = (
        P(("rep", "box"), None, None, None),
        P(("rep", "box"), None, None, None),
        P(("rep", "box")),
        P(("rep", "box")),
        P("segment", None, "box", None),
        P("segment", None),
        P(),
        P(),
    )
    return jax.shard_map(
        functools.partial(per_device, dict(mesh.shape)),
        mesh=mesh,
        in_specs=placed,
        out_specs=P(("rep", "box"), "segment", None),
        check_vma=False,
    )
```

time: 221 us -> 92 us (0.42)
  Pallas kernels: 0 us -> 88.8 us
  waiting for transfers between devices: 85 us -> 0 us
  starting transfers between devices: 65.8 us -> 0 us
  matrix products: 20.2 us -> 0 us
  between operations: 17.3 us -> 0.01 us
  other arithmetic: 13.7 us -> 0 us
  local copies, waits for them, and re-layouts: 11.1 us -> 2.59 us
  blocking collectives: 6.47 us -> 0 us
    pallas_call x0 -> x1, Pallas kernels: none -> 88.8 us  [per_device(): pl.pallas_call(functools.partial(kernel, n_seg, n_rep, n_box, classes), o...]
    ppermute x16 -> x0, starting transfers between devices: 65.8 us -> none  [the longest x12 34.1 us: shifted(): return lax.ppermute(x, axis, pairs)]
    all_gather x1 -> x0, waiting for transfers between devices: 48.1 us -> none  [run_sections(): kernel = lax.all_gather(conv_weights, 'box', axis=2, tiled=True)[0]]
    ppermute x16 -> x0, waiting for transfers between devices: 36.2 us -> none  [the longest x12 35.3 us: shifted(): return lax.ppermute(x, axis, pairs)]
    dot_general x28 -> x0, matrix products: 20.2 us -> none  [the longest x4 7.97 us: convolve(): lax.dot_general(stacked, kernel_cols, (((3,), (0,)), ((), ())), preferred...]
    transpose x1 -> x0, local copies, waits for them, and re-layouts: 6.65 us -> none  [run_sections(): jnp.transpose(kernel, (0, 2, 1)).reshape(9 * channels, channels)]
    all_to_all x1 -> x0, blocking collectives: 6.47 us -> none  [summed_on_arrival(): parts = lax.all_to_all(in_blocks(x, dim, count), axis, 0, 0, tiled=True)]
    abs x1 -> x0, other arithmetic: 5.11 us -> none  [run_sections(): magnitude_cols = jnp.abs(kernel_cols)]
  transfers between devices with their start and end apart: 17 -> 0, of which waited for: 10 -> 0; matrix products, arithmetic and copies ran while one was open for 6% -> 0% of each run, Pallas kernels for 0% -> 0%
where the time goes in v1:
time: 92 us; the launch traced here: 91.4 us
  Pallas kernels  88.8 us (97%)
  local copies, waits for them, and re-layouts  2.59 us (3%)
    pallas_call x1, Pallas kernels, per_device(): pl.pallas_call(functools.partial(kernel, n_seg, n_rep, n_box, classes), o...  88.8 us
    unnamed x2, local copies, waits for them, and re-layouts  2.59 us

profile of v1, /device:TPU:1, one launch (start us, length us, event | category | flops | bytes accessed | tf_op | source)
XLA Modules:
  0.0 91.4 jit_solution(1927629648334575277)
XLA Ops:
  0.0 1.5 %copy.9.hw = bf16[512,10]{1,0:T(8,128)(2,1)} copy(bf16[512,10]{0,1:T(8,128)(2,1)} %param.14) | data formatting | bytes 20480 | tf_op args[6]
  1.5 88.8 %shard_map.82 = f32[1,1,5]{2,1,0:T(1,128)} custom-call(s32[4]{0:T(128)} %cert.1, s32[4]{0:T(128)} %lab.1, f32[4,4,4,512]{3,2,1,0:T(4,128)} %cen.1, f32[4,4,4,512]{3,2,1,0:T(4,128)} %rad.1, bf16[1,9,32,512]{3,2,1,0:T(8,128)(2,1)} %cw.1, f32[1,512]{1,0:T(1,128)} %bias.1, bf16[512,10]{1,0:T(8,128)(2,1)} %copy.9.hw, f32[1,10]{1,0:T(1,128)} %bitcast.1), custom_call_target="tpu_custom_call" | custom-call | tf_op jit(solution)/shard_map/pallas_call | solution.py:376
  90.3 1.1 %copy.11 = f32[1,1,5]{2,1,0:T(1,128)} copy(f32[1,1,5]{2,1,0:T(1,128)} %shard_map.82) | data formatting | bytes 40

commit v2 on v1

v2 whole, which is shorter than its diff:
```python
import functools

import jax
import jax.numpy as jnp
from jax import lax
from jax.experimental import pallas as pl
from jax.experimental.pallas import tpu as pltpu
from jax.sharding import PartitionSpec as P

K = 5
TAPS = 9
TREE = (
    (1, 0), (-1, 0), (3, 0), (-3, 0),
    (2, 3), (-2, -3), (4, 3), (-4, -3), (6, 3), (-6, -3),
    (5, 6), (-5, -6), (7, 6), (-7, -6), (8, 6),
)
FIRST = (1, -1, 3, -3)
HALVED = 0
LAG = 5
LAG2 = 9
bf16 = jnp.bfloat16
f32 = jnp.float32
MESH = pl.DeviceIdType.MESH


def kernel(
    n_seg, n_rep, n_box, classes,
    cert_in, lab_in, cen, rad, cw, bias_in, hw_in, hb_in, out,
    cert, lab, bias, hw, hb, W, S, L, G, C8, R8, PT, MID, fin, fout, cin, cout, CF, NEW, slope, cept, HC, HO, T,
    loc, zs, zr, ys, yr, cs, cr, xs, xr, fs, fr, bs, br, ts, tr,
):
    s = lax.axis_index("segment")
    r = lax.axis_index("rep")
    z = lax.axis_index("box")
    c = lax.rem(r, 2)
    par = lax.rem(r // 2, 2)
    mate = {"rep": r + 1 - 2 * c}
    y_up = {"rep": lax.rem(r + 2, n_rep)}
    y_down = {"rep": lax.rem(r + n_rep - 2, n_rep)}
    jumps = sorted({o - p for o, p in TREE} | {p - o for o, p in TREE})

    def along(o):
        return {"box": lax.rem(z + n_box + o, n_box)}

    peers = []
    for dx in range(n_seg):
        for dc in range(2):
            if dx or dc:
                peers.append(
                    {"segment": lax.rem(s + dx, n_seg), "rep": r + dc * (1 - 2 * c)}
                )
    shard = W.shape[1] // n_box
    half = shard // 2
    rows_y = n_rep // 2
    y = r // 2
    wide = W.shape[2] // 2
    slim = W.shape[2] // rows_y
    mid_tap = HALVED + (TAPS - HALVED) // 2

    own = pltpu.make_async_copy(
        cw.at[0], W.at[:, pl.ds(pl.multiple_of(z * shard, shard), shard), :], loc.at[0]
    )
    own.start()
    own_c = pltpu.make_async_copy(cen, C8.at[pl.ds(4 * c, 4)], loc.at[1])
    own_c.start()
    own_r = pltpu.make_async_copy(rad, R8.at[pl.ds(4 * c, 4)], loc.at[2])
    own_r.start()
    small = []
    for n, (there, here) in enumerate(
        ((cert_in, cert), (lab_in, lab), (bias_in, bias), (hw_in, hw), (hb_in, hb))
    ):
        copy = pltpu.make_async_copy(there, here, loc.at[3 + n])
        copy.start()
        small.append(copy)

    barrier = pltpu.get_barrier_semaphore()
    near = [y_up, y_down] + [along(o) for o in jumps] + peers
    for device in near:
        pl.semaphore_signal(barrier, inc=1, device_id=device, device_id_type=MESH)
    pl.semaphore_wait(barrier, len(near))

    def remote(src, dst, send, recv, device):
        return pltpu.make_async_remote_copy(
            src_ref=src, dst_ref=dst, send_sem=send, recv_sem=recv,
            device_id=device, device_id_type=MESH,
        )

    def piece(n, core, taps, lane, width, back=0):
        b = lax.rem(z + 2 * n_box - TREE[n][0] + back, n_box)
        row = pl.multiple_of(b * shard + core * half, half)
        lane = pl.multiple_of(lane, width)
        return W.at[pl.ds(taps[0], taps[1] - taps[0]), pl.ds(row, half), pl.ds(lane, width)]

    halved, quartered = (0, HALVED), (HALVED, TAPS)
    low_part, high_part = (HALVED, mid_tap), (mid_tap, TAPS)
    y_next, y_prev = lax.rem(y + 1, rows_y), lax.rem(y + rows_y - 1, rows_y)
    y_far = lax.rem(y + 2, rows_y)

    def z_copies(n, arriving=False):
        offset, parent = TREE[n]
        back = 0 if arriving else offset - parent
        out = []
        if HALVED > 0:
            ref = piece(n, c, halved, par * wide, wide, back)
            out.append(remote(ref, ref, zs.at[n, 0], zr.at[n, 0], along(offset - parent)))
        if HALVED < TAPS:
            ref = piece(n, c, quartered, y * slim, slim, back)
            out.append(remote(ref, ref, zs.at[n, 1], zr.at[n, 1], along(offset - parent)))
        return out

    def y_copies(n, arriving=False):
        out = []
        if HALVED > 0:
            side = 1 - par if arriving else par
            ref = piece(n, c, halved, side * wide, wide)
            out.append(remote(ref, ref, ys.at[n, 0], yr.at[n, 0], (y_up, y_down)[n % 2]))
        if HALVED < TAPS:
            for d in range(2):
                part = (y_prev, y_next)[d] if arriving else y
                ref = piece(n, c, quartered, part * slim, slim)
                out.append(remote(ref, ref, ys.at[n, 1 + d], yr.at[n, 1 + d], (y_up, y_down)[d]))
        return out

    def relay_copies(n, arriving=False):
        out = []
        if HALVED < TAPS:
            for d in range(2):
                part = y_far if arriving else (y_prev, y_next)[d]
                ref = piece(n, c, (low_part, high_part)[d], part * slim, slim)
                out.append(remote(ref, ref, ys.at[n, 3 + d], yr.at[n, 3 + d], (y_up, y_down)[d]))
        return out

    def c_copy(n, arriving=False):
        ref = piece(n, 1 - c if arriving else c, (0, TAPS), 0, 2 * wide)
        return remote(ref, ref, cs.at[n], cr.at[n], mate)

    own.wait()
    index = {offset: n for n, (offset, _) in enumerate(TREE)}
    for offset in FIRST:
        for copy in z_copies(index[offset]):
            copy.start()

    own_c.wait()
    own_r.wait()
    for copy in small:
        copy.wait()
    pair_c = remote(C8.at[pl.ds(4 * c, 4)], C8.at[pl.ds(4 * c, 4)], xs.at[0], xr.at[0], mate)
    pair_r = remote(R8.at[pl.ds(4 * c, 4)], R8.at[pl.ds(4 * c, 4)], xs.at[1], xr.at[1], mate)
    row8 = lax.broadcasted_iota(jnp.int32, (8, 128), 0)
    lane8 = lax.broadcasted_iota(jnp.int32, (8, 128), 1)
    tile = jnp.zeros((8, 128), f32)
    for i in range(4):
        alive_i = (1 - cert[i]).astype(f32)
        label_i = lab[i].astype(f32)
        here = lane8 == 4 * c + i
        tile = jnp.where(here & (row8 == 0), alive_i, tile)
        tile = jnp.where(here & (row8 == 1), label_i, tile)
    PT[c] = tile
    pair_t = remote(PT.at[c], PT.at[c], xs.at[2], xr.at[2], mate)
    pair_t.start()
    pair_c.start()
    pair_r.start()

    p_row = lax.broadcasted_iota(jnp.int32, (80, 128), 0)
    p_col = lax.broadcasted_iota(jnp.int32, (80, 128), 1)
    same = (p_row // 16) == (p_col // 16)
    dy = lax.rem(p_col, 16) // 4 - lax.rem(p_row, 16) // 4
    dx_ = lax.rem(p_col, 4) - lax.rem(p_row, 4)
    for t in range(TAPS):
        a, b = divmod(t, 3)
        S[t] = jnp.where(same & (dy == a - 1) & (dx_ == b - 1), 1.0, 0.0).astype(bf16)
    G[...] = jnp.zeros_like(G)

    def take_y(n):
        for copy in y_copies(n, True):
            copy.wait_recv()
        for copy in relay_copies(n):
            copy.start()

    def take_relayed(n):
        for copy in relay_copies(n, True):
            copy.wait_recv()
        c_copy(n).start()

    count = len(TREE)
    for n in range(count + LAG2):
        if n < count:
            for copy in z_copies(n, True):
                copy.wait_recv()
            for child, (_, parent) in enumerate(TREE):
                if parent == TREE[n][0]:
                    for copy in z_copies(child):
                        copy.start()
            for copy in y_copies(n):
                copy.start()
        if 0 <= n - LAG < count:
            take_y(n - LAG)
        if n >= LAG2:
            take_relayed(n - LAG2)

    remote(PT.at[1 - c], PT.at[1 - c], xs.at[2], xr.at[2], mate).wait_recv()
    other = pl.ds(4 * (1 - c), 4)
    remote(C8.at[other], C8.at[other], xs.at[0], xr.at[0], mate).wait_recv()
    remote(R8.at[other], R8.at[other], xs.at[1], xr.at[1], mate).wait_recv()
    both = PT[0] + PT[1]
    alive_row = both[0:1, :]
    label_row = both[1:2, :]
    alive = jnp.sum(jnp.where(lane8 == row8, alive_row, 0.0), axis=1, keepdims=True)
    labels = jnp.sum(jnp.where(lane8 == row8, label_row, 0.0), axis=1, keepdims=True)
    rank = jnp.sum(jnp.where(lane8 < row8, alive_row, 0.0), axis=1, keepdims=True)
    live_no = jnp.where(alive > 0.5, rank, -1.0)
    first = (2 * c).astype(f32)

    @pl.when(s == 0)
    def _():
        for m in range(2):
            pick = jnp.where(live_no == first + m, 1.0, 0.0)
            middle = jnp.zeros((16, C8.shape[3]), f32)
            radius = jnp.zeros((16, C8.shape[3]), f32)
            for i in range(8):
                take = pick[i : i + 1, :] > 0.5
                middle = jnp.where(take, C8[i].reshape(middle.shape), middle)
                radius = jnp.where(take, R8[i].reshape(radius.shape), radius)
            MID[16 * m : 16 * m + 16] = middle
            MID[32 + 16 * m : 48 + 16 * m] = radius

    @pl.when(s == n_seg - 1)
    def _():
        row = lax.broadcasted_iota(jnp.int32, (16, 1), 0)
        spec = lax.rem(row, 8).astype(f32)
        lab0 = jnp.sum(jnp.where(live_no == first, labels, 0.0), axis=0, keepdims=True)
        lab1 = jnp.sum(jnp.where(live_no == first + 1.0, labels, 0.0), axis=0, keepdims=True)
        true = jnp.where(row < 8, lab0, lab1)
        rival = true + 1.0 + spec
        rival = jnp.where(rival >= classes, rival - classes, rival)
        ids = lax.broadcasted_iota(jnp.int32, (16, classes), 1).astype(f32)
        selector = jnp.where(ids == true, 1.0, 0.0) - jnp.where(ids == rival, 1.0, 0.0)
        selector = jnp.where(spec < K, selector, 0.0)
        pooled = lax.dot_general(
            selector.astype(bf16), hw[...], (((1,), (0,)), ((), ())), preferred_element_type=f32
        ) / 16.0
        HC[...] = pooled.reshape(2, 8, pooled.shape[1])
        offset = jnp.sum(selector * hb[...], axis=1, keepdims=True)
        lane16 = lax.broadcasted_iota(jnp.int32, (16, 128), 1)
        HO[...] = jnp.where(lane16 == 0, offset, 0.0)

    for n in range(count):
        c_copy(n, True).wait_recv()

    up_x = {"segment": lax.rem(s + 1, n_seg)}
    down_x = {"segment": lax.rem(s + n_seg - 1, n_seg)}
    part_h = W.shape[1] // 2
    cols = [slice(h * part_h, (h + 1) * part_h) for h in range(2)]

    def f_copy(h):
        return remote(fout.at[h], fin.at[h], fs.at[h], fr.at[h], up_x)

    def b_copy(m, h):
        return remote(cout.at[m, h], cin.at[m, h], bs.at[m, h], br.at[m, h], down_x)

    rows_in = (((1,), (1,)), ((), ()))
    centre = [jnp.zeros((32, part_h), f32) for _ in range(2)]
    spread = [jnp.zeros((32, part_h), f32) for _ in range(2)]
    for h in range(2):
        @pl.when(s > 0)
        def _():
            f_copy(h).wait_recv()
            MID[:, cols[h]] = fin[h].astype(f32)

        G[0:64, cols[h]] = MID[:, cols[h]].astype(bf16)
        for t in range(TAPS):
            L[t, 0:64, cols[h]] = jnp.dot(
                S[t, 0:64], G[:, cols[h]], preferred_element_type=f32
            ).astype(bf16)
        for n in range(2):
            for t in range(TAPS):
                w = W[t, cols[n], cols[h]]
                centre[n] += lax.dot_general(
                    L[t, 0:32, cols[h]], w, rows_in, preferred_element_type=f32
                )
                spread[n] += lax.dot_general(
                    L[t, 32:64, cols[h]], jnp.abs(w), rows_in, preferred_element_type=f32
                )
            if h == 0:
                continue
            middle_n = centre[n] + bias[:, cols[n]]
            low = middle_n - spread[n]
            up = middle_n + spread[n]
            up_pos = jnp.maximum(up, 0.0)
            low_pos = jnp.maximum(low, 0.0)
            low_neg = jnp.maximum(-low, 0.0)
            fout[n, 0:32] = (MID[0:32, cols[n]] + 0.5 * (up_pos + low_pos)).astype(bf16)
            fout[n, 32:64] = (MID[32:64, cols[n]] + 0.5 * (up_pos - low_pos)).astype(bf16)

            @pl.when(s < n_seg - 1)
            def _():
                f_copy(n).start()

            slope_now = up_pos / (up_pos + low_neg)
            cept_now = slope_now * low_neg
            for m in range(2):
                slope[m, :, cols[n]] = slope_now[16 * m : 16 * m + 16]
                cept[m, :, cols[n]] = cept_now[16 * m : 16 * m + 16]

    slot = s * 2 + c
    for m in range(2):
        for h in range(2):
            @pl.when(s == n_seg - 1)
            def _():
                for k in range(K):
                    CF[16 * k : 16 * k + 16, cols[h]] = jnp.broadcast_to(
                        HC[m, k : k + 1, cols[h]], (16, part_h)
                    )

            @pl.when(s < n_seg - 1)
            def _():
                b_copy(m, h).wait_recv()
                CF[:, cols[h]] = cin[m, h].astype(f32)

            slope_m = slope[m, :, cols[h]]
            for k in range(K):
                rows = slice(16 * k, 16 * k + 16)
                G[rows, cols[h]] = (CF[rows, cols[h]] * slope_m).astype(bf16)
            for t in range(TAPS):
                L[t, :, cols[h]] = jnp.dot(
                    S[TAPS - 1 - t], G[:, cols[h]], preferred_element_type=f32
                ).astype(bf16)
            for n in range(2):
                new = NEW[:, cols[n]] if h else jnp.zeros((80, part_h), f32)
                for t in range(TAPS):
                    new += jnp.dot(
                        L[t, :, cols[h]], W[t, cols[h], cols[n]], preferred_element_type=f32
                    )
                if h == 0:
                    NEW[:, cols[n]] = new
                    continue
                new = new + CF[:, cols[n]]
                NEW[:, cols[n]] = new

                @pl.when(s > 0)
                def _():
                    cout[m, n] = new.astype(bf16)
                    b_copy(m, n).start()

        first_section = s == 0
        for k in range(K):
            rows = slice(16 * k, 16 * k + 16)
            now = CF[rows]
            part = now * slope[m] * bias[...] + jnp.minimum(now, 0.0) * cept[m]
            new_k = NEW[rows]
            ends = new_k * MID[16 * m : 16 * m + 16] - jnp.abs(new_k) * MID[
                32 + 16 * m : 48 + 16 * m
            ]
            part = part + jnp.where(first_section, ends, 0.0)
            part = jnp.sum(part, axis=0, keepdims=True)
            folded = part[:, 0:128]
            for q in range(1, part.shape[1] // 128):
                folded = folded + part[:, 128 * q : 128 * q + 128]
            at = 8 * m + k
            folded = folded + jnp.where(s == n_seg - 1, HO[at : at + 1, :], 0.0)
            T[slot, at : at + 1, :] = folded

    sends = []
    for n, device in enumerate(peers):
        copy = remote(T.at[slot], T.at[slot], ts.at[n], tr.at[slot], device)
        copy.start()
        sends.append(copy)
    for dx in range(n_seg):
        for dc in range(2):
            if dx or dc:
                there = lax.rem(s + dx, n_seg) * 2 + c + dc * (1 - 2 * c)
                remote(T.at[there], T.at[there], ts.at[0], tr.at[there], mate).wait_recv()
    mine = jnp.where(row8[:, 0:1] == 4 * c + s, live_no, -1.0)
    mine = jnp.max(mine, axis=0, keepdims=True)
    total = jnp.zeros((8, 128), f32)
    for core in range(2):
        for m in range(2):
            part = T[core, 8 * m : 8 * m + 8]
            for x in range(1, n_seg):
                part = part + T[2 * x + core, 8 * m : 8 * m + 8]
            total = jnp.where((mine == float(2 * core + m)) & (row8 < K), part, total)
    column = jnp.sum(total, axis=1, keepdims=True)
    line = jnp.sum(jnp.where(row8 == lane8, column, 0.0), axis=0, keepdims=True)
    out[0] = line[:, 0:K]

    for copy in sends:
        copy.wait_send()

    for n in range(count):
        for copy in z_copies(n) + y_copies(n) + relay_copies(n):
            copy.wait_send()
        c_copy(n).wait_send()
    pair_c.wait_send()
    pair_r.wait_send()
    pair_t.wait_send()

    @pl.when(s < n_seg - 1)
    def _():
        for h in range(2):
            f_copy(h).wait_send()

    @pl.when(s > 0)
    def _():
        for m in range(2):
            for h in range(2):
                b_copy(m, h).wait_send()


def per_device(mesh_shape, centers, box_radii, labels, certified, conv_weights, conv_bias,
               head_weight, head_bias):
    n_seg, n_rep, n_box = (mesh_shape[a] for a in ("segment", "rep", "box"))
    h = conv_weights.shape[-1]
    classes = head_bias.shape[0]
    dma = pltpu.SemaphoreType.DMA
    vmem = pl.BlockSpec(memory_space=pltpu.VMEM)
    hbm = pl.BlockSpec(memory_space=pl.ANY)
    return pl.pallas_call(
        functools.partial(kernel, n_seg, n_rep, n_box, classes),
        out_shape=jax.ShapeDtypeStruct((1, 1, K), f32),
        in_specs=[hbm] * 8,
        out_specs=vmem,
        scratch_shapes=[
            pltpu.SMEM(certified.shape, jnp.int32),
            pltpu.SMEM(labels.shape, jnp.int32),
            pltpu.VMEM(conv_bias.shape, f32),
            pltpu.VMEM((classes, h), bf16),
            pltpu.VMEM((1, classes), f32),
            pltpu.VMEM((TAPS, h, h), bf16),
            pltpu.VMEM((TAPS, 80, 128), bf16),
            pltpu.VMEM((TAPS, 80, h), bf16),
            pltpu.VMEM((128, h), bf16),
            pltpu.VMEM((8, 4, 4, h), f32),
            pltpu.VMEM((8, 4, 4, h), f32),
            pltpu.VMEM((2, 8, 128), f32),
            pltpu.VMEM((64, h), f32),
            pltpu.VMEM((2, 64, h // 2), bf16),
            pltpu.VMEM((2, 64, h // 2), bf16),
            pltpu.VMEM((2, 2, 80, h // 2), bf16),
            pltpu.VMEM((2, 2, 80, h // 2), bf16),
            pltpu.VMEM((80, h), f32),
            pltpu.VMEM((80, h), f32),
            pltpu.VMEM((2, 16, h), f32),
            pltpu.VMEM((2, 16, h), f32),
            pltpu.VMEM((2, 8, h), f32),
            pltpu.VMEM((16, 128), f32),
            pltpu.VMEM((2 * n_seg, 16, 128), f32),
            dma((8,)),
            dma((len(TREE), 2)),
            dma((len(TREE), 2)),
            dma((len(TREE), 5)),
            dma((len(TREE), 5)),
            dma((len(TREE),)),
            dma((len(TREE),)),
            dma((3,)),
            dma((3,)),
            dma((2,)),
            dma((2,)),
            dma((2, 2)),
            dma((2, 2)),
            dma((2 * n_seg,)),
            dma((2 * n_seg,)),
        ],
        compiler_params=pltpu.CompilerParams(collective_id=0, has_side_effects=True),
    )(certified, labels, centers, box_radii, conv_weights, conv_bias, head_weight.T,
      head_bias[None, :])


def solution(mesh):
    placed = (
        P(("rep", "box"), None, None, None),
        P(("rep", "box"), None, None, None),
        P(("rep", "box")),
        P(("rep", "box")),
        P("segment", None, "box", None),
        P("segment", None),
        P(),
        P(),
    )
    return jax.shard_map(
        functools.partial(per_device, dict(mesh.shape)),
        mesh=mesh,
        in_specs=placed,
        out_specs=P(("rep", "box"), "segment", None),
        check_vma=False,
    )
```

time: 92 us -> 82.6 us (0.90)
  Pallas kernels: 88.8 us -> 80.9 us
  local copies, waits for them, and re-layouts: 2.59 us -> 1.19 us
    pallas_call x1, Pallas kernels: 88.8 us -> 80.9 us  [per_device(): pl.pallas_call(functools.partial(kernel, n_seg, n_rep, n_box, classes), o...]
    unnamed x2 -> x1, local copies, waits for them, and re-layouts: 2.59 us -> 1.19 us
where the time goes in v2:
time: 82.6 us; the launch traced here: 82.1 us
  Pallas kernels  80.9 us (98%)
  local copies, waits for them, and re-layouts  1.19 us (1%)
    pallas_call x1, Pallas kernels, per_device(): pl.pallas_call(functools.partial(kernel, n_seg, n_rep, n_box, classes), o...  80.9 us

profile of v2, /device:TPU:1, one launch (start us, length us, event | category | flops | bytes accessed | tf_op | source)
XLA Modules:
  0.0 82.1 jit_solution(3931609432409180928)
XLA Ops:
  0.0 80.9 %shard_map.82 = f32[1,1,5]{2,1,0:T(1,128)} custom-call(s32[4]{0:T(128)} %cert_in.1, s32[4]{0:T(128)} %lab_in.1, f32[4,4,4,512]{3,2,1,0:T(4,128)} %cen.1, f32[4,4,4,512]{3,2,1,0:T(4,128)} %rad.1, bf16[1,9,32,512]{3,2,1,0:T(8,128)(2,1)} %cw.1, f32[1,512]{1,0:T(1,128)} %bias_in.1, bf16[10,512]{1,0:T(8,128)(2,1)} %bitcast.2, f32[1,10]{1,0:T(1,128)} %bitcast.3), custom_call_target="tpu_custom_call" | custom-call | tf_op jit(solution)/shard_map/pallas_call | solution.py:417
  80.9 1.2 %copy.10 = f32[1,1,5]{2,1,0:T(1,128)} copy(f32[1,1,5]{2,1,0:T(1,128)} %shard_map.82) | data formatting | bytes 40

commit v3 on v2

--- a/solution.py
+++ b/solution.py
@@ -10,12 +10,11 @@
 K = 5
 TAPS = 9
 TREE = (
-    (1, 0), (-1, 0), (3, 0), (-3, 0),
-    (2, 3), (-2, -3), (4, 3), (-4, -3), (6, 3), (-6, -3),
-    (5, 6), (-5, -6), (7, 6), (-7, -6), (8, 6),
+    (1, 0), (-1, 0), (2, 0), (-2, 0),
+    (3, 2), (-3, -2), (4, 2), (-4, -2), (5, 4), (-5, -4), (6, 4), (-6, -4),
+    (7, 6), (-7, -6), (8, 6),
 )
-FIRST = (1, -1, 3, -3)
-HALVED = 0
+FIRST = (1, -1, 2, -2)
 LAG = 5
 LAG2 = 9
 bf16 = jnp.bfloat16
@@ -26,14 +25,13 @@
 def kernel(
     n_seg, n_rep, n_box, classes,
     cert_in, lab_in, cen, rad, cw, bias_in, hw_in, hb_in, out,
-    cert, lab, bias, hw, hb, W, S, L, G, C8, R8, PT, MID, fin, fout, cin, cout, CF, NEW, slope, cept, HC, HO, T,
+    cert, lab, bias, hw, hb, W, S, L, G, C8, R8, PT, MID, fin, fout, cin, cout, CF, NEW, ACC, slope, cept, HC, HO, T,
     loc, zs, zr, ys, yr, cs, cr, xs, xr, fs, fr, bs, br, ts, tr,
 ):
     s = lax.axis_index("segment")
     r = lax.axis_index("rep")
     z = lax.axis_index("box")
     c = lax.rem(r, 2)
-    par = lax.rem(r // 2, 2)
     mate = {"rep": r + 1 - 2 * c}
     y_up = {"rep": lax.rem(r + 2, n_rep)}
     y_down = {"rep": lax.rem(r + n_rep - 2, n_rep)}
@@ -55,7 +53,7 @@
     y = r // 2
     wide = W.shape[2] // 2
     slim = W.shape[2] // rows_y
-    mid_tap = HALVED + (TAPS - HALVED) // 2
+    mid_tap = TAPS // 2
 
     own = pltpu.make_async_copy(
         cw.at[0], W.at[:, pl.ds(pl.multiple_of(z * shard, shard), shard), :], loc.at[0]
@@ -91,54 +89,42 @@
         lane = pl.multiple_of(lane, width)
         return W.at[pl.ds(taps[0], taps[1] - taps[0]), pl.ds(row, half), pl.ds(lane, width)]
 
-    halved, quartered = (0, HALVED), (HALVED, TAPS)
-    low_part, high_part = (HALVED, mid_tap), (mid_tap, TAPS)
+    every, low_part, high_part = (0, TAPS), (0, mid_tap), (mid_tap, TAPS)
     y_next, y_prev = lax.rem(y + 1, rows_y), lax.rem(y + rows_y - 1, rows_y)
     y_far = lax.rem(y + 2, rows_y)
 
-    def z_copies(n, arriving=False):
+    def z_copy(n, arriving=False):
         offset, parent = TREE[n]
-        back = 0 if arriving else offset - parent
-        out = []
-        if HALVED > 0:
-            ref = piece(n, c, halved, par * wide, wide, back)
-            out.append(remote(ref, ref, zs.at[n, 0], zr.at[n, 0], along(offset - parent)))
-        if HALVED < TAPS:
-            ref = piece(n, c, quartered, y * slim, slim, back)
-            out.append(remote(ref, ref, zs.at[n, 1], zr.at[n, 1], along(offset - parent)))
-        return out
+        ref = piece(n, c, every, y * slim, slim, 0 if arriving else offset - parent)
+        return remote(ref, ref, zs.at[n], zr.at[n], along(offset - parent))
 
     def y_copies(n, arriving=False):
         out = []
-        if HALVED > 0:
-            side = 1 - par if arriving else par
-            ref = piece(n, c, halved, side * wide, wide)
-            out.append(remote(ref, ref, ys.at[n, 0], yr.at[n, 0], (y_up, y_down)[n % 2]))
-        if HALVED < TAPS:
-            for d in range(2):
-                part = (y_prev, y_next)[d] if arriving else y
-                ref = piece(n, c, quartered, part * slim, slim)
-                out.append(remote(ref, ref, ys.at[n, 1 + d], yr.at[n, 1 + d], (y_up, y_down)[d]))
+        for d in range(2):
+            part = (y_prev, y_next)[d] if arriving else y
+            ref = piece(n, c, every, part * slim, slim)
+            out.append(remote(ref, ref, ys.at[n, d], yr.at[n, d], (y_up, y_down)[d]))
         return out
 
     def relay_copies(n, arriving=False):
         out = []
-        if HALVED < TAPS:
-            for d in range(2):
-                part = y_far if arriving else (y_prev, y_next)[d]
-                ref = piece(n, c, (low_part, high_part)[d], part * slim, slim)
-                out.append(remote(ref, ref, ys.at[n, 3 + d], yr.at[n, 3 + d], (y_up, y_down)[d]))
+        for d in range(2):
+            part = y_far if arriving else (y_prev, y_next)[d]
+            ref = piece(n, c, (low_part, high_part)[d], part * slim, slim)
+            out.append(remote(ref, ref, ys.at[n, 2 + d], yr.at[n, 2 + d], (y_up, y_down)[d]))
         return out
 
-    def c_copy(n, arriving=False):
-        ref = piece(n, 1 - c if arriving else c, (0, TAPS), 0, 2 * wide)
-        return remote(ref, ref, cs.at[n], cr.at[n], mate)
+    near_half = y // 2
+
+    def c_copy(n, far, arriving=False):
+        side = 1 - near_half if far else near_half
+        ref = piece(n, 1 - c if arriving else c, every, side * wide, wide)
+        return remote(ref, ref, cs.at[n, far], cr.at[n, far], mate)
 
     own.wait()
     index = {offset: n for n, (offset, _) in enumerate(TREE)}
     for offset in FIRST:
-        for copy in z_copies(index[offset]):
-            copy.start()
+        z_copy(index[offset]).start()
 
     own_c.wait()
     own_r.wait()
@@ -171,30 +157,27 @@
         S[t] = jnp.where(same & (dy == a - 1) & (dx_ == b - 1), 1.0, 0.0).astype(bf16)
     G[...] = jnp.zeros_like(G)
 
-    def take_y(n):
-        for copy in y_copies(n, True):
-            copy.wait_recv()
-        for copy in relay_copies(n):
-            copy.start()
+    count = len(TREE)
 
     def take_relayed(n):
         for copy in relay_copies(n, True):
             copy.wait_recv()
-        c_copy(n).start()
-
-    count = len(TREE)
-    for n in range(count + LAG2):
+        c_copy(n, 1).start()
+
+    for n in range(count + LAG):
         if n < count:
-            for copy in z_copies(n, True):
-                copy.wait_recv()
+            z_copy(n, True).wait_recv()
             for child, (_, parent) in enumerate(TREE):
                 if parent == TREE[n][0]:
-                    for copy in z_copies(child):
-                        copy.start()
+                    z_copy(child).start()
             for copy in y_copies(n):
                 copy.start()
-        if 0 <= n - LAG < count:
-            take_y(n - LAG)
+        if n >= LAG:
+            for copy in y_copies(n - LAG, True):
+                copy.wait_recv()
+            for copy in relay_copies(n - LAG):
+                copy.start()
+            c_copy(n - LAG, 0).start()
         if n >= LAG2:
             take_relayed(n - LAG2)
 
@@ -244,13 +227,11 @@
         lane16 = lax.broadcasted_iota(jnp.int32, (16, 128), 1)
         HO[...] = jnp.where(lane16 == 0, offset, 0.0)
 
-    for n in range(count):
-        c_copy(n, True).wait_recv()
-
     up_x = {"segment": lax.rem(s + 1, n_seg)}
     down_x = {"segment": lax.rem(s + n_seg - 1, n_seg)}
     part_h = W.shape[1] // 2
     cols = [slice(h * part_h, (h + 1) * part_h) for h in range(2)]
+    rows_in = (((1,), (1,)), ((), ()))
 
     def f_copy(h):
         return remote(fout.at[h], fin.at[h], fs.at[h], fr.at[h], up_x)
@@ -258,34 +239,31 @@
     def b_copy(m, h):
         return remote(cout.at[m, h], cin.at[m, h], bs.at[m, h], br.at[m, h], down_x)
 
-    rows_in = (((1,), (1,)), ((), ()))
-    centre = [jnp.zeros((32, part_h), f32) for _ in range(2)]
-    spread = [jnp.zeros((32, part_h), f32) for _ in range(2)]
-    for h in range(2):
-        @pl.when(s > 0)
-        def _():
-            f_copy(h).wait_recv()
-            MID[:, cols[h]] = fin[h].astype(f32)
-
-        G[0:64, cols[h]] = MID[:, cols[h]].astype(bf16)
+    def half_forward(h, finish):
+        here = pl.ds(pl.multiple_of(h * part_h, part_h), part_h)
+        G[0:64, here] = MID[:, here].astype(bf16)
         for t in range(TAPS):
-            L[t, 0:64, cols[h]] = jnp.dot(
-                S[t, 0:64], G[:, cols[h]], preferred_element_type=f32
+            L[t, 0:64, here] = jnp.dot(
+                S[t, 0:64], G[:, here], preferred_element_type=f32
             ).astype(bf16)
         for n in range(2):
+            start = ACC[n] if finish else jnp.zeros((64, part_h), f32)
+            centre, spread = start[0:32], start[32:64]
             for t in range(TAPS):
-                w = W[t, cols[n], cols[h]]
-                centre[n] += lax.dot_general(
-                    L[t, 0:32, cols[h]], w, rows_in, preferred_element_type=f32
+                w = W[t, cols[n], here]
+                centre += lax.dot_general(
+                    L[t, 0:32, here], w, rows_in, preferred_element_type=f32
                 )
-                spread[n] += lax.dot_general(
-                    L[t, 32:64, cols[h]], jnp.abs(w), rows_in, preferred_element_type=f32
+                spread += lax.dot_general(
+                    L[t, 32:64, here], jnp.abs(w), rows_in, preferred_element_type=f32
                 )
-            if h == 0:
+            if not finish:
+                ACC[n, 0:32] = centre
+                ACC[n, 32:64] = spread
                 continue
-            middle_n = centre[n] + bias[:, cols[n]]
-            low = middle_n - spread[n]
-            up = middle_n + spread[n]
+            centre = centre + bias[:, cols[n]]
+            low = centre - spread
+            up = centre + spread
             up_pos = jnp.maximum(up, 0.0)
             low_pos = jnp.maximum(low, 0.0)
             low_neg = jnp.maximum(-low, 0.0)
@@ -302,56 +280,40 @@
                 slope[m, :, cols[n]] = slope_now[16 * m : 16 * m + 16]
                 cept[m, :, cols[n]] = cept_now[16 * m : 16 * m + 16]
 
+    for n in range(count):
+        c_copy(n, 0, True).wait_recv()
+
+    @pl.when(s == 0)
+    def _():
+        half_forward(near_half, False)
+
+    for n in range(count + LAG - LAG2, count):
+        take_relayed(n)
+    for n in range(count):
+        c_copy(n, 1, True).wait_recv()
+
+    @pl.when(s > 0)
+    def _():
+        f_copy(0).wait_recv()
+        MID[:, cols[0]] = fin[0].astype(f32)
+        half_forward(0, False)
+        f_copy(1).wait_recv()
+        MID[:, cols[1]] = fin[1].astype(f32)
+
+    half_forward(jnp.where(s == 0, 1 - near_half, 1), True)
+
     slot = s * 2 + c
-    for m in range(2):
-        for h in range(2):
-            @pl.when(s == n_seg - 1)
-            def _():
-                for k in range(K):
-                    CF[16 * k : 16 * k + 16, cols[h]] = jnp.broadcast_to(
-                        HC[m, k : k + 1, cols[h]], (16, part_h)
-                    )
-
-            @pl.when(s < n_seg - 1)
-            def _():
-                b_copy(m, h).wait_recv()
-                CF[:, cols[h]] = cin[m, h].astype(f32)
-
-            slope_m = slope[m, :, cols[h]]
-            for k in range(K):
-                rows = slice(16 * k, 16 * k + 16)
-                G[rows, cols[h]] = (CF[rows, cols[h]] * slope_m).astype(bf16)
-            for t in range(TAPS):
-                L[t, :, cols[h]] = jnp.dot(
-                    S[TAPS - 1 - t], G[:, cols[h]], preferred_element_type=f32
-                ).astype(bf16)
-            for n in range(2):
-                new = NEW[:, cols[n]] if h else jnp.zeros((80, part_h), f32)
-                for t in range(TAPS):
-                    new += jnp.dot(
-                        L[t, :, cols[h]], W[t, cols[h], cols[n]], preferred_element_type=f32
-                    )
-                if h == 0:
-                    NEW[:, cols[n]] = new
-                    continue
-                new = new + CF[:, cols[n]]
-                NEW[:, cols[n]] = new
-
-                @pl.when(s > 0)
-                def _():
-                    cout[m, n] = new.astype(bf16)
-                    b_copy(m, n).start()
-
-        first_section = s == 0
+
+    def terms(m):
         for k in range(K):
             rows = slice(16 * k, 16 * k + 16)
-            now = CF[rows]
+            now = CF[m, rows]
             part = now * slope[m] * bias[...] + jnp.minimum(now, 0.0) * cept[m]
-            new_k = NEW[rows]
+            new_k = NEW[m, rows]
             ends = new_k * MID[16 * m : 16 * m + 16] - jnp.abs(new_k) * MID[
                 32 + 16 * m : 48 + 16 * m
             ]
-            part = part + jnp.where(first_section, ends, 0.0)
+            part = part + jnp.where(s == 0, ends, 0.0)
             part = jnp.sum(part, axis=0, keepdims=True)
             folded = part[:, 0:128]
             for q in range(1, part.shape[1] // 128):
@@ -359,6 +321,51 @@
             at = 8 * m + k
             folded = folded + jnp.where(s == n_seg - 1, HO[at : at + 1, :], 0.0)
             T[slot, at : at + 1, :] = folded
+
+    for m in range(2):
+        for h in range(2):
+            @pl.when(s == n_seg - 1)
+            def _():
+                for k in range(K):
+                    CF[m, 16 * k : 16 * k + 16, cols[h]] = jnp.broadcast_to(
+                        HC[m, k : k + 1, cols[h]], (16, part_h)
+                    )
+
+            @pl.when(s < n_seg - 1)
+            def _():
+                b_copy(m, h).wait_recv()
+                CF[m, :, cols[h]] = cin[m, h].astype(f32)
+
+            slope_m = slope[m, :, cols[h]]
+            for k in range(K):
+                rows = slice(16 * k, 16 * k + 16)
+                G[rows, cols[h]] = (CF[m, rows, cols[h]] * slope_m).astype(bf16)
+            for t in range(TAPS):
+                L[t, :, cols[h]] = jnp.dot(
+                    S[TAPS - 1 - t], G[:, cols[h]], preferred_element_type=f32
+                ).astype(bf16)
+            for n in range(2):
+                new = NEW[m, :, cols[n]] if h else jnp.zeros((80, part_h), f32)
+                for t in range(TAPS):
+                    new += jnp.dot(
+                        L[t, :, cols[h]], W[t, cols[h], cols[n]], preferred_element_type=f32
+                    )
+                if h == 0:
+                    NEW[m, :, cols[n]] = new
+                    continue
+                new = new + CF[m, :, cols[n]]
+                NEW[m, :, cols[n]] = new
+
+                @pl.when(s > 0)
+                def _():
+                    cout[m, n] = new.astype(bf16)
+                    b_copy(m, n).start()
+
+        if m == 0:
+            pl.when(s == 0)(functools.partial(terms, 0))
+
+    pl.when(s > 0)(functools.partial(terms, 0))
+    terms(1)
 
     sends = []
     for n, device in enumerate(peers):
@@ -387,9 +394,10 @@
         copy.wait_send()
 
     for n in range(count):
-        for copy in z_copies(n) + y_copies(n) + relay_copies(n):
+        for copy in [z_copy(n)] + y_copies(n) + relay_copies(n):
             copy.wait_send()
-        c_copy(n).wait_send()
+        for far in range(2):
+            c_copy(n, far).wait_send()
     pair_c.wait_send()
     pair_r.wait_send()
     pair_t.wait_send()
@@ -437,20 +445,21 @@
             pltpu.VMEM((2, 64, h // 2), bf16),
             pltpu.VMEM((2, 2, 80, h // 2), bf16),
             pltpu.VMEM((2, 2, 80, h // 2), bf16),
-            pltpu.VMEM((80, h), f32),
-            pltpu.VMEM((80, h), f32),
+            pltpu.VMEM((2, 80, h), f32),
+            pltpu.VMEM((2, 80, h), f32),
+            pltpu.VMEM((2, 64, h // 2), f32),
             pltpu.VMEM((2, 16, h), f32),
             pltpu.VMEM((2, 16, h), f32),
             pltpu.VMEM((2, 8, h), f32),
             pltpu.VMEM((16, 128), f32),
             pltpu.VMEM((2 * n_seg, 16, 128), f32),
             dma((8,)),
+            dma((len(TREE),)),
+            dma((len(TREE),)),
+            dma((len(TREE), 4)),
+            dma((len(TREE), 4)),
             dma((len(TREE), 2)),
             dma((len(TREE), 2)),
-            dma((len(TREE), 5)),
-            dma((len(TREE), 5)),
-            dma((len(TREE),)),
-            dma((len(TREE),)),
             dma((3,)),
             dma((3,)),
             dma((2,)),

time: 82.6 us -> 81.2 us (0.983)
  Pallas kernels: 80.9 us -> 79.5 us
    pallas_call x1, Pallas kernels: 80.9 us -> 79.5 us  [per_device(): pl.pallas_call(functools.partial(kernel, n_seg, n_rep, n_box, classes), o...]
where the time goes in v3:
time: 81.2 us; the launch traced here: 80.7 us
  Pallas kernels  79.5 us (98%)
  local copies, waits for them, and re-layouts  1.19 us (1%)
    pallas_call x1, Pallas kernels, per_device(): pl.pallas_call(functools.partial(kernel, n_seg, n_rep, n_box, classes), o...  79.5 us

profile of v3, /device:TPU:1, one launch (start us, length us, event | category | flops | bytes accessed | tf_op | source)
XLA Modules:
  0.0 80.7 jit_solution(15935187603876676585)
XLA Ops:
  0.0 79.5 %shard_map.82 = f32[1,1,5]{2,1,0:T(1,128)} custom-call(s32[4]{0:T(128)} %cert_in.1, s32[4]{0:T(128)} %lab_in.1, f32[4,4,4,512]{3,2,1,0:T(4,128)} %cen.1, f32[4,4,4,512]{3,2,1,0:T(4,128)} %rad.1, bf16[1,9,32,512]{3,2,1,0:T(8,128)(2,1)} %cw.1, f32[1,512]{1,0:T(1,128)} %bias_in.1, bf16[10,512]{1,0:T(8,128)(2,1)} %bitcast.2, f32[1,10]{1,0:T(1,128)} %bitcast.3), custom_call_target="tpu_custom_call" | custom-call | tf_op jit(solution)/shard_map/pallas_call | solution.py:425
  79.5 1.2 %copy.10 = f32[1,1,5]{2,1,0:T(1,128)} copy(f32[1,1,5]{2,1,0:T(1,128)} %shard_map.82) | data formatting | bytes 40

commit v4 on v3

--- a/solution.py
+++ b/solution.py
@@ -9,12 +9,9 @@
 
 K = 5
 TAPS = 9
-TREE = (
-    (1, 0), (-1, 0), (2, 0), (-2, 0),
-    (3, 2), (-3, -2), (4, 2), (-4, -2), (5, 4), (-5, -4), (6, 4), (-6, -4),
-    (7, 6), (-7, -6), (8, 6),
-)
-FIRST = (1, -1, 2, -2)
+TREE = ((2,0),(-2,0),(4,2),(-4,-2),(3,2),(-3,-2),(6,4),(-6,-4),(5,4),(-5,-4),(8,6),(7,6),(-7,-6),(1,0),(-1,0))
+FIRST = (2,-2,1,-1)
+WHOLE = (1, -1)
 LAG = 5
 LAG2 = 9
 bf16 = jnp.bfloat16
@@ -86,7 +83,7 @@
     def piece(n, core, taps, lane, width, back=0):
         b = lax.rem(z + 2 * n_box - TREE[n][0] + back, n_box)
         row = pl.multiple_of(b * shard + core * half, half)
-        lane = pl.multiple_of(lane, width)
+        lane = pl.multiple_of(lane, width) if width < 2 * wide else 0
         return W.at[pl.ds(taps[0], taps[1] - taps[0]), pl.ds(row, half), pl.ds(lane, width)]
 
     every, low_part, high_part = (0, TAPS), (0, mid_tap), (mid_tap, TAPS)
@@ -95,12 +92,14 @@
 
     def z_copy(n, arriving=False):
         offset, parent = TREE[n]
-        ref = piece(n, c, every, y * slim, slim, 0 if arriving else offset - parent)
+        back = 0 if arriving else offset - parent
+        lane, width = (0, 2 * wide) if offset in WHOLE else (y * slim, slim)
+        ref = piece(n, c, every, lane, width, back)
         return remote(ref, ref, zs.at[n], zr.at[n], along(offset - parent))
 
     def y_copies(n, arriving=False):
         out = []
-        for d in range(2):
+        for d in () if TREE[n][0] in WHOLE else range(2):
             part = (y_prev, y_next)[d] if arriving else y
             ref = piece(n, c, every, part * slim, slim)
             out.append(remote(ref, ref, ys.at[n, d], yr.at[n, d], (y_up, y_down)[d]))
@@ -108,7 +107,7 @@
 
     def relay_copies(n, arriving=False):
         out = []
-        for d in range(2):
+        for d in () if TREE[n][0] in WHOLE else range(2):
             part = y_far if arriving else (y_prev, y_next)[d]
             ref = piece(n, c, (low_part, high_part)[d], part * slim, slim)
             out.append(remote(ref, ref, ys.at[n, 2 + d], yr.at[n, 2 + d], (y_up, y_down)[d]))
@@ -162,7 +161,8 @@
     def take_relayed(n):
         for copy in relay_copies(n, True):
             copy.wait_recv()
-        c_copy(n, 1).start()
+        if TREE[n][0] not in WHOLE:
+            c_copy(n, 1).start()
 
     for n in range(count + LAG):
         if n < count:
@@ -172,12 +172,16 @@
                     z_copy(child).start()
             for copy in y_copies(n):
                 copy.start()
+            if TREE[n][0] in WHOLE:
+                for far in range(2):
+                    c_copy(n, far).start()
         if n >= LAG:
             for copy in y_copies(n - LAG, True):
                 copy.wait_recv()
             for copy in relay_copies(n - LAG):
                 copy.start()
-            c_copy(n - LAG, 0).start()
+            if TREE[n - LAG][0] not in WHOLE:
+                c_copy(n - LAG, 0).start()
         if n >= LAG2:
             take_relayed(n - LAG2)
 

time: 81.2 us -> 80.6 us (level)
  no operation moved by 1% of the time
where the time goes in v4:
time: 80.6 us; the launch traced here: 80.1 us
  Pallas kernels  78.9 us (98%)
  local copies, waits for them, and re-layouts  1.19 us (1%)
    pallas_call x1, Pallas kernels, per_device(): pl.pallas_call(functools.partial(kernel, n_seg, n_rep, n_box, classes), o...  78.9 us

profile of v4, /device:TPU:1, one launch (start us, length us, event | category | flops | bytes accessed | tf_op | source)
XLA Modules:
  0.0 80.1 jit_solution(688350081888789377)
XLA Ops:
  0.0 78.9 %shard_map.82 = f32[1,1,5]{2,1,0:T(1,128)} custom-call(s32[4]{0:T(128)} %cert_in.1, s32[4]{0:T(128)} %lab_in.1, f32[4,4,4,512]{3,2,1,0:T(4,128)} %cen.1, f32[4,4,4,512]{3,2,1,0:T(4,128)} %rad.1, bf16[1,9,32,512]{3,2,1,0:T(8,128)(2,1)} %cw.1, f32[1,512]{1,0:T(1,128)} %bias_in.1, bf16[10,512]{1,0:T(8,128)(2,1)} %bitcast.2, f32[1,10]{1,0:T(1,128)} %bitcast.3), custom_call_target="tpu_custom_call" | custom-call | tf_op jit(solution)/shard_map/pallas_call | solution.py:429
  78.9 1.2 %copy.10 = f32[1,1,5]{2,1,0:T(1,128)} copy(f32[1,1,5]{2,1,0:T(1,128)} %shard_map.82) | data formatting | bytes 40

commit v5 on v4

--- a/solution.py
+++ b/solution.py
@@ -376,6 +376,26 @@
         copy = remote(T.at[slot], T.at[slot], ts.at[n], tr.at[slot], device)
         copy.start()
         sends.append(copy)
+    for n in range(count):
+        for copy in [z_copy(n)] + y_copies(n) + relay_copies(n):
+            copy.wait_send()
+        for far in range(2):
+            c_copy(n, far).wait_send()
+    pair_c.wait_send()
+    pair_r.wait_send()
+    pair_t.wait_send()
+
+    @pl.when(s < n_seg - 1)
+    def _():
+        for h in range(2):
+            f_copy(h).wait_send()
+
+    @pl.when(s > 0)
+    def _():
+        for m in range(2):
+            for h in range(2):
+                b_copy(m, h).wait_send()
+
     for dx in range(n_seg):
         for dc in range(2):
             if dx or dc:
@@ -393,29 +413,8 @@
     column = jnp.sum(total, axis=1, keepdims=True)
     line = jnp.sum(jnp.where(row8 == lane8, column, 0.0), axis=0, keepdims=True)
     out[0] = line[:, 0:K]
-
     for copy in sends:
         copy.wait_send()
-
-    for n in range(count):
-        for copy in [z_copy(n)] + y_copies(n) + relay_copies(n):
-            copy.wait_send()
-        for far in range(2):
-            c_copy(n, far).wait_send()
-    pair_c.wait_send()
-    pair_r.wait_send()
-    pair_t.wait_send()
-
-    @pl.when(s < n_seg - 1)
-    def _():
-        for h in range(2):
-            f_copy(h).wait_send()
-
-    @pl.when(s > 0)
-    def _():
-        for m in range(2):
-            for h in range(2):
-                b_copy(m, h).wait_send()
 
 
 def per_device(mesh_shape, centers, box_radii, labels, certified, conv_weights, conv_bias,

time: 80.6 us -> 80.5 us (level)
  no operation moved by 1% of the time
where the time goes in v5:
time: 80.5 us; the launch traced here: 79.9 us
  Pallas kernels  78.7 us (98%)
  local copies, waits for them, and re-layouts  1.19 us (1%)
    pallas_call x1, Pallas kernels, per_device(): pl.pallas_call(functools.partial(kernel, n_seg, n_rep, n_box, classes), o...  78.7 us

profile of v5, /device:TPU:1, one launch (start us, length us, event | category | flops | bytes accessed | tf_op | source)
XLA Modules:
  0.0 79.9 jit_solution(8902094193436985140)
XLA Ops:
  0.0 78.7 %shard_map.82 = f32[1,1,5]{2,1,0:T(1,128)} custom-call(s32[4]{0:T(128)} %cert_in.1, s32[4]{0:T(128)} %lab_in.1, f32[4,4,4,512]{3,2,1,0:T(4,128)} %cen.1, f32[4,4,4,512]{3,2,1,0:T(4,128)} %rad.1, bf16[1,9,32,512]{3,2,1,0:T(8,128)(2,1)} %cw.1, f32[1,512]{1,0:T(1,128)} %bias_in.1, bf16[10,512]{1,0:T(8,128)(2,1)} %bitcast.2, f32[1,10]{1,0:T(1,128)} %bitcast.3), custom_call_target="tpu_custom_call" | custom-call | tf_op jit(solution)/shard_map/pallas_call | solution.py:428
  78.7 1.2 %copy.10 = f32[1,1,5]{2,1,0:T(1,128)} copy(f32[1,1,5]{2,1,0:T(1,128)} %shard_map.82) | data formatting | bytes 40

commit v6 on v5

--- a/solution.py
+++ b/solution.py
@@ -243,13 +243,16 @@
     def b_copy(m, h):
         return remote(cout.at[m, h], cin.at[m, h], bs.at[m, h], br.at[m, h], down_x)
 
-    def half_forward(h, finish):
+    def windows(h):
         here = pl.ds(pl.multiple_of(h * part_h, part_h), part_h)
         G[0:64, here] = MID[:, here].astype(bf16)
         for t in range(TAPS):
             L[t, 0:64, here] = jnp.dot(
                 S[t, 0:64], G[:, here], preferred_element_type=f32
             ).astype(bf16)
+
+    def half_forward(h, finish):
+        here = pl.ds(pl.multiple_of(h * part_h, part_h), part_h)
         for n in range(2):
             start = ACC[n] if finish else jnp.zeros((64, part_h), f32)
             centre, spread = start[0:32], start[32:64]
@@ -289,7 +292,9 @@
 
     @pl.when(s == 0)
     def _():
+        windows(near_half)
         half_forward(near_half, False)
+        windows(1 - near_half)
 
     for n in range(count + LAG - LAG2, count):
         take_relayed(n)
@@ -300,9 +305,11 @@
     def _():
         f_copy(0).wait_recv()
         MID[:, cols[0]] = fin[0].astype(f32)
+        windows(0)
         half_forward(0, False)
         f_copy(1).wait_recv()
         MID[:, cols[1]] = fin[1].astype(f32)
+        windows(1)
 
     half_forward(jnp.where(s == 0, 1 - near_half, 1), True)
 

time: 80.5 us -> 81 us (level)
  no operation moved by 1% of the time
where the time goes in v6:
time: 81 us; the launch traced here: 80.5 us
  Pallas kernels  79.3 us (98%)
  local copies, waits for them, and re-layouts  1.19 us (1%)
    pallas_call x1, Pallas kernels, per_device(): pl.pallas_call(functools.partial(kernel, n_seg, n_rep, n_box, classes), o...  79.3 us

profile of v6, /device:TPU:1, one launch (start us, length us, event | category | flops | bytes accessed | tf_op | source)
XLA Modules:
  0.0 80.5 jit_solution(16882348266221673128)
XLA Ops:
  0.0 79.3 %shard_map.82 = f32[1,1,5]{2,1,0:T(1,128)} custom-call(s32[4]{0:T(128)} %cert_in.1, s32[4]{0:T(128)} %lab_in.1, f32[4,4,4,512]{3,2,1,0:T(4,128)} %cen.1, f32[4,4,4,512]{3,2,1,0:T(4,128)} %rad.1, bf16[1,9,32,512]{3,2,1,0:T(8,128)(2,1)} %cw.1, f32[1,512]{1,0:T(1,128)} %bias_in.1, bf16[10,512]{1,0:T(8,128)(2,1)} %bitcast.2, f32[1,10]{1,0:T(1,128)} %bitcast.3), custom_call_target="tpu_custom_call" | custom-call | tf_op jit(solution)/shard_map/pallas_call | solution.py:435
  79.3 1.2 %copy.10 = f32[1,1,5]{2,1,0:T(1,128)} copy(f32[1,1,5]{2,1,0:T(1,128)} %shard_map.82) | data formatting | bytes 40
